TPU v7x, 256 devices: a whole 4x4x8 slice. The times are simulated.
256 devices in a mesh: tile: 32 (over x_lo, z, core), mlp: 8 (over y, x_hi).
Axes of the slice: x: 4 (x_hi: 2, x_lo: 2; x = x_hi * 2 + x_lo), y: 4, z: 8, core: 2. Of those that a mesh axis runs over, the one named last changes fastest.
Arguments:
- features: bfloat16 [32, 512, 2, 2, 256], P('tile', 'mlp'), may hold values from -6 to 6
- w_in: bfloat16 [256, 1024], P(None, 'mlp'), may hold values from -0.375 to 0.375
- w_out: bfloat16 [1024, 256], P('mlp'), may hold values from -0.1875 to 0.1875
- bilinear: bfloat16 [256, 256], replicated, may hold values from -0.375 to 0.375
- partner: int32 [32, 2, 512], replicated, may hold values from 0 to 13823
- counts: int32 [32, 2, 2], replicated, may hold values from 128 to 512
Outputs:
- pair_loss: float32 [], replicated
- grad_in: float32 [256, 1024], P(None, 'mlp')
- grad_out: float32 [1024, 256], P('mlp')
- grad_bilinear: float32 [256, 256], replicated
All inputs are finite; a program needn't handle non-finite values.
Results may differ from a plain program's by a relative error of at most 0.0024.
The roundings to bfloat16 on the way count: a program that leaves them out, or rounds other values in their place, can miss the bound.
Values may be sent and summed in bfloat16 or wider, within the bound.
A program may use at most 64 MiB of HBM per device.

v0:
```python
import jax
import jax.numpy as jnp
from jax import lax
from jax.sharding import PartitionSpec as P

column_plan = ((-1, 1), (0, 0), (0, 1), (1, 0))


def shifted(array, axis, by):
    peers = lax.axis_size(axis)
    pairs = [(i, i + by) for i in range(peers) if 0 <= i + by < peers]
    return lax.ppermute(array, axis, pairs)


def pair_slope(raw_score, target, weight, heavy_weight, factor):
    chance = jax.nn.sigmoid(raw_score)
    signed = (1.0 - target) * chance - heavy_weight * target * (1.0 - chance)
    return (weight * signed * factor).astype(jnp.bfloat16)


def pair_cost(raw_score, target, weight, heavy_weight):
    missed = heavy_weight * target * jnp.log1p(jnp.exp(-raw_score))
    spurious = (1.0 - target) * jnp.log1p(jnp.exp(raw_score))
    return jnp.sum(weight * (missed + spurious))


def local(features, w_in, w_out, bilinear, partner, counts):
    row_part = features.shape[1]
    feature_width = features.shape[4]
    groups = lax.axis_size("mlp")
    site_rows = row_part * groups
    tile_count = lax.axis_size("tile")
    grid_depth = tile_count // 8
    tile_here = lax.axis_index("tile")
    member = lax.axis_index("mlp")
    block_x = tile_here // (4 * grid_depth)
    block_y = tile_here // grid_depth % 4
    block_z = tile_here % grid_depth
    heavy_weight = 27 * site_rows // 4
    score_scale = feature_width ** (-0.5)
    factor = score_scale / (2 * tile_count * site_rows)
    own_rows = member * row_part + jnp.arange(row_part, dtype=jnp.int32)
    all_rows = jnp.arange(site_rows, dtype=jnp.int32)
    mine_counts = lax.dynamic_index_in_dim(counts, tile_here, 0, keepdims=False)
    mine_partner = lax.dynamic_index_in_dim(partner, tile_here, 0, keepdims=False)
    own_partner = lax.dynamic_slice_in_dim(mine_partner, member * row_part, row_part, 1)
    own_pre_ok = own_rows[None, :] < mine_counts[:, 0:1]
    own_post_ok = own_rows[None, :] < mine_counts[:, 1:2]
    local_x = features.reshape(row_part, 4, feature_width)
    whole_x = lax.all_gather(local_x, "mlp", axis=0, tiled=True)
    hidden_pre = jnp.einsum("rcf,fh->rch", whole_x, w_in, preferred_element_type=jnp.float32)
    active = jax.nn.gelu(hidden_pre).astype(jnp.bfloat16)
    mixed_rows = lax.psum_scatter(
        jnp.einsum("rch,hf->rcf", active, w_out, preferred_element_type=jnp.float32),
        "mlp",
        scatter_dimension=0,
        tiled=True,
    )
    embedded = (local_x.astype(jnp.float32) + mixed_rows).astype(jnp.bfloat16)
    pre_local = embedded[:, 0::2]
    post_local = embedded[:, 1::2]
    query_local = jnp.einsum(
        "ruf,fg->rug", pre_local, bilinear, preferred_element_type=jnp.float32
    ).astype(jnp.bfloat16)

    def pair_code(step_x, step_y, step_z):
        return ((step_x + 1) * 9 + (step_y + 1) * 3 + step_z + 1) * site_rows

    loss_sum = jnp.zeros((), jnp.float32)
    post_grads = [
        jnp.zeros((row_part, feature_width), jnp.float32),
        jnp.zeros((row_part, feature_width), jnp.float32),
    ]
    post_whole, query_whole = (
        lax.all_gather(post_local, "mlp", axis=0, tiled=True),
        lax.all_gather(query_local, "mlp", axis=0, tiled=True),
    )
    query_grads = [
        jnp.zeros((row_part, feature_width), jnp.float32),
        jnp.zeros((row_part, feature_width), jnp.float32),
    ]
    for step_y in (-1, 0, 1):
        for step_z in (-1, 0, 1):
            post_cols, query_cols, post_valid, pre_valid, label_cols = ([], [], [], [], [])
            for position in range(4):
                shift_x, sub_tile = column_plan[position]
                offset = shift_x * 4 * grid_depth + step_y * grid_depth + step_z
                inside = (
                    (block_x + shift_x >= 0)
                    & (block_x + shift_x < 2)
                    & (block_y + step_y >= 0)
                    & (block_y + step_y < 4)
                    & (block_z + step_z >= 0)
                    & (block_z + step_z < grid_depth)
                )
                source = jnp.clip(tile_here + offset, 0, tile_count - 1)
                tile_counts = lax.dynamic_index_in_dim(counts, source, 0, keepdims=False)[sub_tile]
                labels = lax.dynamic_index_in_dim(partner, source, 0, keepdims=False)[sub_tile]
                offset, sub_tile, inside, tile_counts, labels = (
                    offset,
                    sub_tile,
                    inside,
                    tile_counts,
                    labels,
                )
                both_sides = jnp.stack([post_whole[:, sub_tile], query_whole[:, sub_tile]], 0)
                if offset != 0:
                    both_sides = shifted(both_sides, "tile", -offset)
                post_cols.append(both_sides[0])
                query_cols.append(both_sides[1])
                post_valid.append(inside & (all_rows < tile_counts[1]))
                pre_valid.append(inside & (all_rows < tile_counts[0]))
                label_cols.append(labels)
            for pretile in (0, 1):
                chosen = range(pretile, pretile + 3)
                others = jnp.concatenate([post_cols[column_id] for column_id in chosen], 0)
                col_key = jnp.concatenate(
                    [
                        pair_code(column_id - 1 - pretile, step_y, step_z) + all_rows
                        for column_id in chosen
                    ]
                )
                col_ok = jnp.concatenate([post_valid[column_id] for column_id in chosen])
                raw_score = (
                    jnp.einsum(
                        "rf,cf->rc",
                        query_local[:, pretile],
                        others,
                        preferred_element_type=jnp.float32,
                    )
                    * score_scale
                )
                target = (own_partner[pretile][:, None] == col_key[None, :]).astype(jnp.float32)
                weight = (own_pre_ok[pretile][:, None] & col_ok[None, :]).astype(jnp.float32)
                loss_sum = loss_sum + pair_cost(raw_score, target, weight, heavy_weight)
                slope = pair_slope(raw_score, target, weight, heavy_weight, factor)
                query_grads[pretile] = query_grads[pretile] + jnp.dot(
                    slope, others, preferred_element_type=jnp.float32
                )
                senders = jnp.concatenate([query_cols[column_id] for column_id in chosen], 0)
                row_key = jnp.concatenate(
                    [
                        label_cols[column_id] - pair_code(pretile - column_id + 1, -step_y, -step_z)
                        for column_id in chosen
                    ]
                )
                row_ok = jnp.concatenate([pre_valid[column_id] for column_id in chosen])
                back_score = (
                    jnp.einsum(
                        "cf,rf->cr",
                        post_local[:, pretile],
                        senders,
                        preferred_element_type=jnp.float32,
                    )
                    * score_scale
                )
                back_target = (own_rows[:, None] == row_key[None, :]).astype(jnp.float32)
                back_weight = (own_post_ok[pretile][:, None] & row_ok[None, :]).astype(jnp.float32)
                back_slope = pair_slope(back_score, back_target, back_weight, heavy_weight, factor)
                post_grads[pretile] = post_grads[pretile] + jnp.dot(
                    back_slope, senders, preferred_element_type=jnp.float32
                )
    query_total = jnp.stack(query_grads, 1)
    query_back = query_total.astype(jnp.bfloat16)
    post_back = jnp.stack(post_grads, 1)
    bilinear_part = jnp.einsum(
        "ruf,rug->fg", pre_local, query_back, preferred_element_type=jnp.float32
    )
    pre_back = jnp.einsum("rug,fg->ruf", query_back, bilinear, preferred_element_type=jnp.float32)
    embed_grad = jnp.stack(
        [pre_back[:, 0], post_back[:, 0], pre_back[:, 1], post_back[:, 1]], 1
    ).astype(jnp.bfloat16)
    embed_whole = lax.all_gather(embed_grad, "mlp", axis=0, tiled=True)
    active_grad = jnp.einsum("rcf,hf->rch", embed_whole, w_out, preferred_element_type=jnp.float32)
    unused, pullback = jax.vjp(jax.nn.gelu, hidden_pre)
    hidden_grad = pullback(active_grad)[0].astype(jnp.bfloat16)
    in_part = jnp.einsum("rcf,rch->fh", whole_x, hidden_grad, preferred_element_type=jnp.float32)
    out_part = jnp.einsum("rch,rcf->hf", active, embed_whole, preferred_element_type=jnp.float32)
    grad_in, grad_out = lax.psum((in_part, out_part), "tile")
    grad_bilinear, loss_total = lax.psum((bilinear_part, loss_sum), ("tile", "mlp"))
    pair_loss = loss_total / (2.0 * tile_count * site_rows * 27 * site_rows)
    return (pair_loss, grad_in, grad_out, grad_bilinear)


def solution(mesh):
    placed = (P("tile", "mlp", None, None, None), P(None, "mlp"), P("mlp", None), P(), P(), P())
    return jax.shard_map(
        local,
        mesh=mesh,
        in_specs=placed,
        out_specs=(P(), P(None, "mlp"), P("mlp", None), P()),
        check_vma=False,
    )
```

profile of v0, /device:TPU:2, one launch (start us, length us, event | category | flops | bytes accessed | tf_op | source)
XLA Modules:
  0.0 1315.0 jit_solution(17551962125909204225)
XLA Ops:
  7.2 1.6 copy.14
  9.6 2.7 constant_dynamic-slice_fusion.65
  32.2 1.8 constant_dynamic-slice_fusion.77
  69.1 1.6 fusion.714
  70.8 1.8 fusion.712
  85.1 70.2 %reduce-scatter.2.cloned.1.call-done = f32[64,4,256]{2,0,1:T(8,128)} async-done(((f32[512,4,256]{2,0,1:T(8,128)}), f32[64,4,256]{2,0,1:T(8,128)}) %reduce-scatter.2.cloned.1.call-update) | async-done | bytes 262160 | tf_op jit(solution)/shard_map/reduce_scatter | solution.py:53
  156.3 35.8 %all_gather.13 = bf16[512,2,256]{2,0,1:T(8,128)(2,1)S(1)} all-gather(bf16[64,2,256]{2,0,1:T(8,128)(2,1)S(1)} %slice.1000), channel_id=1, replica_groups=mesh['tile'=32,'mlp'=8] {'mlp'}, dimensions={0}, use_global_device_ids=true | all-gather | bytes 589824 | tf_op jit(solution)/shard_map/all_gather | solution.py:75
  192.4 35.4 %all_gather.14 = bf16[512,2,256]{2,0,1:T(8,128)(2,1)S(1)} all-gather(bf16[64,2,256]{2,0,1:T(8,128)(2,1)S(1)} %convolution_convert_fusion.1), channel_id=1, replica_groups=mesh['tile'=32,'mlp'=8] {'mlp'}, dimensions={0}, use_global_device_ids=true | all-gather | bytes 589824 | tf_op jit(solution)/shard_map/all_gather | solution.py:76
  228.0 4.5 collective-permute-start.5
  233.2 5.8 collective-permute-start.6
  241.5 1.9 collective-permute-start.1
  243.4 2.9 collective-permute-start.2
  246.3 8.3 collective-permute-done.5
  255.3 33.1 %collective-permute-done.6 = bf16[2,512,256]{2,1,0:T(8,128)(2,1)S(1)} collective-permute-done((bf16[2,512,256]{2,1,0:T(8,128)(2,1)S(1)}, bf16[2,512,256]{2,1,0:T(8,128)(2,1)S(1)}, u32[]{:S(2)}, u32[]{:S(2)}) %collective-permute-start.6) | collective-permute-done | bytes 524320 | tf_op jit(solution)/shard_map/ppermute | solution.py:12
  288.4 6.2 collective-permute-start.9
  294.6 9.4 collective-permute-start.10
  304.8 26.9 %collective-permute-done.2 = bf16[2,512,256]{2,1,0:T(8,128)(2,1)S(1)} collective-permute-done((bf16[2,512,256]{2,1,0:T(8,128)(2,1)S(1)}, bf16[2,512,256]{2,1,0:T(8,128)(2,1)S(1)}, u32[]{:S(2)}, u32[]{:S(2)}) %collective-permute-start.2) | collective-permute-done | bytes 524320 | tf_op jit(solution)/shard_map/ppermute | solution.py:12
  331.8 12.9 collective-permute-start.13
  344.7 1.9 collective-permute-start.14
  348.1 14.5 %collective-permute-done.10 = bf16[2,512,256]{2,1,0:T(8,128)(2,1)S(1)} collective-permute-done((bf16[2,512,256]{2,1,0:T(8,128)(2,1)S(1)}, bf16[2,512,256]{2,1,0:T(8,128)(2,1)S(1)}, u32[]{:S(2)}, u32[]{:S(2)}) %collective-permute-start.10) | collective-permute-done | bytes 524320 | tf_op jit(solution)/shard_map/ppermute | solution.py:12
  364.6 37.0 %collective-permute-start.19 = (bf16[2,512,256]{2,1,0:T(8,128)(2,1)S(1)}, bf16[2,512,256]{2,1,0:T(8,128)(2,1)S(1)}, u32[]{:S(2)}, u32[]{:S(2)}) collective-permute-start(bf16[2,512,256]{2,1,0:T(8,128)(2,1)S(1)} %pad_maximum_fusion.37), channel_id=1, source_target_pairs={{8,0},{16,8},{24,16},{32,24},{40,32},{48,40},{56,48},{64,56},{72,6... | collective-permute-start | bytes 1572872 | tf_op jit(solution)/shard_map/ppermute | solution.py:12
  402.5 3.3 collective-permute-start.20
  406.5 34.3 %collective-permute-start.18 = (bf16[2,512,256]{2,1,0:T(8,128)(2,1)S(1)}, bf16[2,512,256]{2,1,0:T(8,128)(2,1)S(1)}, u32[]{:S(2)}, u32[]{:S(2)}) collective-permute-start(bf16[2,512,256]{2,1,0:T(8,128)(2,1)S(1)} %pad_maximum_fusion.36), channel_id=1, source_target_pairs={{0,120},{8,128},{16,136},{24,144},{32,152},{40,160},{48,168},{56,1... | collective-permute-start | bytes 1572872 | tf_op jit(solution)/shard_map/ppermute | solution.py:12
  441.6 6.8 collective-permute-start.23
  449.2 5.2 collective-permute-start.24
  455.1 4.5 collective-permute-start.22
  460.3 6.4 collective-permute-done.23
  466.7 4.2 collective-permute-start.27
  471.6 25.0 %collective-permute-done.24 = bf16[2,512,256]{2,1,0:T(8,128)(2,1)S(1)} collective-permute-done((bf16[2,512,256]{2,1,0:T(8,128)(2,1)S(1)}, bf16[2,512,256]{2,1,0:T(8,128)(2,1)S(1)}, u32[]{:S(2)}, u32[]{:S(2)}) %collective-permute-start.24) | collective-permute-done | bytes 524320 | tf_op jit(solution)/shard_map/ppermute | solution.py:12
  496.7 1.9 collective-permute-start.28
  499.3 16.6 %collective-permute-done.22 = bf16[2,512,256]{2,1,0:T(8,128)(2,1)S(1)} collective-permute-done((bf16[2,512,256]{2,1,0:T(8,128)(2,1)S(1)}, bf16[2,512,256]{2,1,0:T(8,128)(2,1)S(1)}, u32[]{:S(2)}, u32[]{:S(2)}) %collective-permute-start.22) | collective-permute-done | bytes 524320 | tf_op jit(solution)/shard_map/ppermute | solution.py:12
  517.4 20.6 %collective-permute-done.27 = bf16[2,512,256]{2,1,0:T(8,128)(2,1)S(1)} collective-permute-done((bf16[2,512,256]{2,1,0:T(8,128)(2,1)S(1)}, bf16[2,512,256]{2,1,0:T(8,128)(2,1)S(1)}, u32[]{:S(2)}, u32[]{:S(2)}) %collective-permute-start.27) | collective-permute-done | bytes 524320 | tf_op jit(solution)/shard_map/ppermute | solution.py:12
  538.0 1.9 collective-permute-start.26
  542.8 12.0 collective-permute-done.28
  554.9 1.9 collective-permute-start.31
  559.7 14.3 %collective-permute-done.26 = bf16[2,512,256]{2,1,0:T(8,128)(2,1)S(1)} collective-permute-done((bf16[2,512,256]{2,1,0:T(8,128)(2,1)S(1)}, bf16[2,512,256]{2,1,0:T(8,128)(2,1)S(1)}, u32[]{:S(2)}, u32[]{:S(2)}) %collective-permute-start.26) | collective-permute-done | bytes 524320 | tf_op jit(solution)/shard_map/ppermute | solution.py:12
  574.0 27.5 %collective-permute-start.32 = (bf16[2,512,256]{2,1,0:T(8,128)(2,1)S(1)}, bf16[2,512,256]{2,1,0:T(8,128)(2,1)S(1)}, u32[]{:S(2)}, u32[]{:S(2)}) collective-permute-start(bf16[2,512,256]{2,1,0:T(8,128)(2,1)S(1)} %pad_maximum_fusion.36), channel_id=1, source_target_pairs={{40,0},{48,8},{56,16},{64,24},{72,32},{80,40},{88,48},{96,56},{104... | collective-permute-start | bytes 1572872 | tf_op jit(solution)/shard_map/ppermute | solution.py:12
  602.6 28.6 %collective-permute-start.30 = (bf16[2,512,256]{2,1,0:T(8,128)(2,1)S(1)}, bf16[2,512,256]{2,1,0:T(8,128)(2,1)S(1)}, u32[]{:S(2)}, u32[]{:S(2)}) collective-permute-start(bf16[2,512,256]{2,1,0:T(8,128)(2,1)S(1)} %pad_maximum_fusion.36), channel_id=1, source_target_pairs={{0,88},{8,96},{16,104},{24,112},{32,120},{40,128},{48,136},{56,144... | collective-permute-start | bytes 1572872 | tf_op jit(solution)/shard_map/ppermute | solution.py:12
  632.3 1.9 collective-permute-start.7
  637.1 3.7 collective-permute-start.3
  642.1 16.8 %collective-permute-done.7 = bf16[2,512,256]{2,1,0:T(8,128)(2,1)S(1)} collective-permute-done((bf16[2,512,256]{2,1,0:T(8,128)(2,1)S(1)}, bf16[2,512,256]{2,1,0:T(8,128)(2,1)S(1)}, u32[]{:S(2)}, u32[]{:S(2)}) %collective-permute-start.7) | collective-permute-done | bytes 524320 | tf_op jit(solution)/shard_map/ppermute | solution.py:12
  658.9 13.2 %collective-permute-start.15 = (bf16[2,512,256]{2,1,0:T(8,128)(2,1)S(1)}, bf16[2,512,256]{2,1,0:T(8,128)(2,1)S(1)}, u32[]{:S(2)}, u32[]{:S(2)}) collective-permute-start(bf16[2,512,256]{2,1,0:T(8,128)(2,1)S(1)} %pad_maximum_fusion.37), channel_id=1, source_target_pairs={{120,0},{128,8},{136,16},{144,24},{152,32},{160,40},{168,48},{176,... | collective-permute-start | bytes 1572872 | tf_op jit(solution)/shard_map/ppermute | solution.py:12
  673.3 3.4 fusion.103
  676.7 21.2 %collective-permute-start.17 = (bf16[2,512,256]{2,1,0:T(8,128)(2,1)S(1)}, bf16[2,512,256]{2,1,0:T(8,128)(2,1)S(1)}, u32[]{:S(2)}, u32[]{:S(2)}) collective-permute-start(bf16[2,512,256]{2,1,0:T(8,128)(2,1)S(1)} %pad_maximum_fusion.37), channel_id=1, source_target_pairs={{128,0},{136,8},{144,16},{152,24},{160,32},{168,40},{176,48},{184,... | collective-permute-start | bytes 1572872 | tf_op jit(solution)/shard_map/ppermute | solution.py:12
  700.1 1.9 collective-permute-start.11
  709.5 3.4 fusion.97
  715.2 2.9 collective-permute-done.11
  718.8 3.5 fusion.109
  726.2 1.9 fusion.365
  728.1 2.5 fusion.364
  730.6 2.1 convolution_add_fusion.15
  732.7 2.3 convolution_add_fusion.7
  735.1 2.1 convolution_add_fusion.14
  737.2 2.2 convolution_add_fusion.6
  739.4 2.1 convolution_add_fusion.13
  753.4 70.2 %all-gather.5.cloned.1.call-done = bf16[512,4,256]{2,0,1:T(8,128)(2,1)} async-done(((bf16[64,4,256]{2,0,1:T(8,128)(2,1)}), bf16[512,4,256]{2,0,1:T(8,128)(2,1)}) %all-gather.5.cloned.1.call-update) | async-done | bytes 1048592 | tf_op jit(solution)/shard_map/all_gather | solution.py:173
  823.5 2.5 convolution_bitcast_fusion.1
  826.0 1.7 convolution_bitcast_fusion.2
  840.1 75.1 %psum.28 = f32[]{:T(128)} all-reduce(f32[]{:T(128)S(6)} %add.976), channel_id=1, replica_groups=mesh['tile'=32,'mlp'=8] {'tile','mlp'}, use_global_device_ids=true, to_apply=%region_19.20 | all-reduce | flops 1 | bytes 8 | tf_op jit(solution)/shard_map/psum | solution.py:180
  915.8 131.6 %all-reduce.6.cloned.1.call-done = (f32[256,128]{0,1:T(8,128)}, f32[128,256]{1,0:T(8,128)}) async-done(((f32[256,128]{0,1:T(8,128)}, f32[128,256]{1,0:T(8,128)}), (f32[256,128]{0,1:T(8,128)}, f32[128,256]{1,0:T(8,128)})) %all-reduce.6.cloned.1.call-update) | async-done | bytes 262160 | tf_op jit(solution)/shard_map/psum | solution.py:179
  1047.4 1.7 copy.17
  1049.0 254.7 %all-reduce.4.cloned.1.call-done = f32[256,256]{1,0:T(8,128)} async-done(((f32[256,256]{1,0:T(8,128)}), f32[256,256]{1,0:T(8,128)}) %all-reduce.4.cloned.1.call-update) | async-done | bytes 262160 | tf_op jit(solution)/shard_map/psum | solution.py:180
  1303.7 1.6 copy.23
  1305.3 1.7 copy.24
  (430 shorter events, 126.0 us)
Async XLA Ops:
  7.2 185.1 %copy-start = (bf16[256,256]{1,0:T(8,128)(2,1)S(1)}, bf16[256,256]{1,0:T(8,128)(2,1)}, u32[]{:S(2)}) copy-start(bf16[256,256]{1,0:T(8,128)(2,1)} %param.9) | copy-start | bytes 393220
  7.2 61.9 %copy-start.31 = (bf16[256,128]{1,0:T(8,128)(2,1)S(1)}, bf16[256,128]{1,0:T(8,128)(2,1)}, u32[]{:S(2)}) copy-start(bf16[256,128]{1,0:T(8,128)(2,1)} %param.7) | copy-start | bytes 196612
  7.2 61.9 %all-gather.3.cloned.1.call-start = ((), (), s32[]{:S(2)}) async-start(), calls=%async_computation.1 | async-start | bytes 1179648 | tf_op jit(solution)/shard_map/all_gather | solution.py:50
  8.9 146.5 %reduce-scatter.2.cloned.1.call-start = ((), (), s32[]{:S(2)}) async-start(), calls=%async_computation.2 | async-start | bytes 2359296 | tf_op jit(solution)/shard_map/reduce_scatter | solution.py:53
  9.2 61.6 %copy-start.32 = (bf16[128,256]{1,0:T(8,128)(2,1)S(1)}, bf16[128,256]{1,0:T(8,128)(2,1)}, u32[]{:S(2)}) copy-start(bf16[128,256]{1,0:T(8,128)(2,1)} %param.8) | copy-start | bytes 196612
  72.6 82.7 %copy-start.1 = (bf16[1,64,2,2,256]{4,1,3,2,0:T(8,128)(2,1)S(1)}, bf16[1,64,2,2,256]{4,1,3,2,0:T(8,128)(2,1)}, u32[]{:S(2)}) copy-start(bf16[1,64,2,2,256]{4,1,3,2,0:T(8,128)(2,1)} %copy.14) | copy-start | bytes 393220
  72.6 750.9 %all-gather.5.cloned.1.call-start = ((), (), s32[]{:S(2)}) async-start(), calls=%async_computation.3 | async-start | bytes 1179648 | tf_op jit(solution)/shard_map/all_gather | solution.py:173
  72.7 119.6 %copy-start.84 = (s32[64]{0:T(128)}, s32[64]{0:T(128)S(1)}, u32[]{:S(2)}) copy-start(s32[64]{0:T(128)S(1)} %iota_add_fusion.26) | copy-start | bytes 772
  73.3 636.1 %copy-start.51 = (s32[1536]{0:T(1024)}, s32[1536]{0:T(1024)S(1)}, u32[]{:S(2)}) copy-start(s32[1536]{0:T(1024)S(1)} %pad_add_fusion) | copy-start | bytes 18436
  73.3 629.8 %copy-start.45 = (s32[1536]{0:T(1024)}, s32[1536]{0:T(1024)S(1)}, u32[]{:S(2)}) copy-start(s32[1536]{0:T(1024)S(1)} %pad_add_fusion.2) | copy-start | bytes 18436
  73.4 630.2 %copy-start.43 = (s32[1536]{0:T(1024)}, s32[1536]{0:T(1024)S(1)}, u32[]{:S(2)}) copy-start(s32[1536]{0:T(1024)S(1)} %pad_add_fusion.3) | copy-start | bytes 18436
  73.4 631.9 %copy-start.41 = (s32[1536]{0:T(1024)}, s32[1536]{0:T(1024)S(1)}, u32[]{:S(2)}) copy-start(s32[1536]{0:T(1024)S(1)} %pad_add_fusion.4) | copy-start | bytes 18436
  73.5 640.6 %copy-start.37 = (s32[1536]{0:T(1024)}, s32[1536]{0:T(1024)S(1)}, u32[]{:S(2)}) copy-start(s32[1536]{0:T(1024)S(1)} %pad_add_fusion.8) | copy-start | bytes 18436
  228.0 26.6 %collective-permute-start.5 = (bf16[2,512,256]{2,1,0:T(8,128)(2,1)S(1)}, bf16[2,512,256]{2,1,0:T(8,128)(2,1)S(1)}, u32[]{:S(2)}, u32[]{:S(2)}) collective-permute-start(bf16[2,512,256]{2,1,0:T(8,128)(2,1)S(1)} %pad_maximum_fusion.37), channel_id=1, source_target_pairs={{0,32},{8,40},{16,48},{24,56},{32,64},{40,72},{48,80},{56,88},{64,... | collective-permute-start | bytes 1572872 | tf_op jit(solution)/shard_map/ppermute | solution.py:12
  233.2 55.2 %collective-permute-start.6 = (bf16[2,512,256]{2,1,0:T(8,128)(2,1)S(1)}, bf16[2,512,256]{2,1,0:T(8,128)(2,1)S(1)}, u32[]{:S(2)}, u32[]{:S(2)}) collective-permute-start(bf16[2,512,256]{2,1,0:T(8,128)(2,1)S(1)} %pad_maximum_fusion.36), channel_id=1, source_target_pairs={{0,32},{8,40},{16,48},{24,56},{32,64},{40,72},{48,80},{56,88},{64,... | collective-permute-start | bytes 1572872 | tf_op jit(solution)/shard_map/ppermute | solution.py:12
  240.2 54.4 %collective-permute-start.4 = (bf16[2,512,256]{2,1,0:T(8,128)(2,1)S(1)}, bf16[2,512,256]{2,1,0:T(8,128)(2,1)S(1)}, u32[]{:S(2)}, u32[]{:S(2)}) collective-permute-start(bf16[2,512,256]{2,1,0:T(8,128)(2,1)S(1)} %pad_maximum_fusion.36), channel_id=1, source_target_pairs={{0,160},{8,168},{16,176},{24,184},{32,192},{40,200},{48,208},{56,2... | collective-permute-start | bytes 1572872 | tf_op jit(solution)/shard_map/ppermute | solution.py:12
  241.5 62.6 %collective-permute-start.1 = (bf16[2,512,256]{2,1,0:T(8,128)(2,1)S(1)}, bf16[2,512,256]{2,1,0:T(8,128)(2,1)S(1)}, u32[]{:S(2)}, u32[]{:S(2)}) collective-permute-start(bf16[2,512,256]{2,1,0:T(8,128)(2,1)S(1)} %pad_maximum_fusion.37), channel_id=1, source_target_pairs={{0,40},{8,48},{16,56},{24,64},{32,72},{40,80},{48,88},{56,96},{64,... | collective-permute-start | bytes 1572872 | tf_op jit(solution)/shard_map/ppermute | solution.py:12
  243.4 88.4 %collective-permute-start.2 = (bf16[2,512,256]{2,1,0:T(8,128)(2,1)S(1)}, bf16[2,512,256]{2,1,0:T(8,128)(2,1)S(1)}, u32[]{:S(2)}, u32[]{:S(2)}) collective-permute-start(bf16[2,512,256]{2,1,0:T(8,128)(2,1)S(1)} %pad_maximum_fusion.36), channel_id=1, source_target_pairs={{0,40},{8,48},{16,56},{24,64},{32,72},{40,80},{48,88},{56,96},{64,... | collective-permute-start | bytes 1572872 | tf_op jit(solution)/shard_map/ppermute | solution.py:12
  254.6 90.1 %collective-permute-start = (bf16[2,512,256]{2,1,0:T(8,128)(2,1)S(1)}, bf16[2,512,256]{2,1,0:T(8,128)(2,1)S(1)}, u32[]{:S(2)}, u32[]{:S(2)}) collective-permute-start(bf16[2,512,256]{2,1,0:T(8,128)(2,1)S(1)} %pad_maximum_fusion.36), channel_id=1, source_target_pairs={{0,168},{8,176},{16,184},{24,192},{32,200},{40,208},{48,216},{56,2... | collective-permute-start | bytes 1572872 | tf_op jit(solution)/shard_map/ppermute | solution.py:12
  288.4 59.0 %collective-permute-start.9 = (bf16[2,512,256]{2,1,0:T(8,128)(2,1)S(1)}, bf16[2,512,256]{2,1,0:T(8,128)(2,1)S(1)}, u32[]{:S(2)}, u32[]{:S(2)}) collective-permute-start(bf16[2,512,256]{2,1,0:T(8,128)(2,1)S(1)} %pad_maximum_fusion.37), channel_id=1, source_target_pairs={{0,24},{8,32},{16,40},{24,48},{32,56},{40,64},{48,72},{56,80},{64,... | collective-permute-start | bytes 1572872 | tf_op jit(solution)/shard_map/ppermute | solution.py:12
  294.6 68.0 %collective-permute-start.10 = (bf16[2,512,256]{2,1,0:T(8,128)(2,1)S(1)}, bf16[2,512,256]{2,1,0:T(8,128)(2,1)S(1)}, u32[]{:S(2)}, u32[]{:S(2)}) collective-permute-start(bf16[2,512,256]{2,1,0:T(8,128)(2,1)S(1)} %pad_maximum_fusion.36), channel_id=1, source_target_pairs={{0,24},{8,32},{16,40},{24,48},{32,56},{40,64},{48,72},{56,80},{64,... | collective-permute-start | bytes 1572872 | tf_op jit(solution)/shard_map/ppermute | solution.py:12
  304.1 60.6 %collective-permute-start.8 = (bf16[2,512,256]{2,1,0:T(8,128)(2,1)S(1)}, bf16[2,512,256]{2,1,0:T(8,128)(2,1)S(1)}, u32[]{:S(2)}, u32[]{:S(2)}) collective-permute-start(bf16[2,512,256]{2,1,0:T(8,128)(2,1)S(1)} %pad_maximum_fusion.36), channel_id=1, source_target_pairs={{0,152},{8,160},{16,168},{24,176},{32,184},{40,192},{48,200},{56,2... | collective-permute-start | bytes 1572872 | tf_op jit(solution)/shard_map/ppermute | solution.py:12
  331.8 70.7 %collective-permute-start.13 = (bf16[2,512,256]{2,1,0:T(8,128)(2,1)S(1)}, bf16[2,512,256]{2,1,0:T(8,128)(2,1)S(1)}, u32[]{:S(2)}, u32[]{:S(2)}) collective-permute-start(bf16[2,512,256]{2,1,0:T(8,128)(2,1)S(1)} %pad_maximum_fusion.37), channel_id=1, source_target_pairs={{0,8},{8,16},{16,24},{24,32},{32,40},{40,48},{48,56},{56,64},{64,7... | collective-permute-start | bytes 1572872 | tf_op jit(solution)/shard_map/ppermute | solution.py:12
  344.7 61.8 %collective-permute-start.14 = (bf16[2,512,256]{2,1,0:T(8,128)(2,1)S(1)}, bf16[2,512,256]{2,1,0:T(8,128)(2,1)S(1)}, u32[]{:S(2)}, u32[]{:S(2)}) collective-permute-start(bf16[2,512,256]{2,1,0:T(8,128)(2,1)S(1)} %pad_maximum_fusion.36), channel_id=1, source_target_pairs={{0,8},{8,16},{16,24},{24,32},{32,40},{40,48},{48,56},{56,64},{64,7... | collective-permute-start | bytes 1572872 | tf_op jit(solution)/shard_map/ppermute | solution.py:12
  347.4 284.9 %collective-permute-start.12 = (bf16[2,512,256]{2,1,0:T(8,128)(2,1)S(1)}, bf16[2,512,256]{2,1,0:T(8,128)(2,1)S(1)}, u32[]{:S(2)}, u32[]{:S(2)}) collective-permute-start(bf16[2,512,256]{2,1,0:T(8,128)(2,1)S(1)} %pad_maximum_fusion.36), channel_id=1, source_target_pairs={{0,136},{8,144},{16,152},{24,160},{32,168},{40,176},{48,184},{56,1... | collective-permute-start | bytes 1572872 | tf_op jit(solution)/shard_map/ppermute | solution.py:12
  362.6 272.7 %collective-permute-start.16 = (bf16[2,512,256]{2,1,0:T(8,128)(2,1)S(1)}, bf16[2,512,256]{2,1,0:T(8,128)(2,1)S(1)}, u32[]{:S(2)}, u32[]{:S(2)}) collective-permute-start(bf16[2,512,256]{2,1,0:T(8,128)(2,1)S(1)} %pad_maximum_fusion.36), channel_id=1, source_target_pairs={{0,128},{8,136},{16,144},{24,152},{32,160},{40,168},{48,176},{56,1... | collective-permute-start | bytes 1572872 | tf_op jit(solution)/shard_map/ppermute | solution.py:12
  364.6 77.0 %collective-permute-start.19 = (bf16[2,512,256]{2,1,0:T(8,128)(2,1)S(1)}, bf16[2,512,256]{2,1,0:T(8,128)(2,1)S(1)}, u32[]{:S(2)}, u32[]{:S(2)}) collective-permute-start(bf16[2,512,256]{2,1,0:T(8,128)(2,1)S(1)} %pad_maximum_fusion.37), channel_id=1, source_target_pairs={{8,0},{16,8},{24,16},{32,24},{40,32},{48,40},{56,48},{64,56},{72,6... | collective-permute-start | bytes 1572872 | tf_op jit(solution)/shard_map/ppermute | solution.py:12
  402.5 46.7 %collective-permute-start.20 = (bf16[2,512,256]{2,1,0:T(8,128)(2,1)S(1)}, bf16[2,512,256]{2,1,0:T(8,128)(2,1)S(1)}, u32[]{:S(2)}, u32[]{:S(2)}) collective-permute-start(bf16[2,512,256]{2,1,0:T(8,128)(2,1)S(1)} %pad_maximum_fusion.36), channel_id=1, source_target_pairs={{8,0},{16,8},{24,16},{32,24},{40,32},{48,40},{56,48},{64,56},{72,6... | collective-permute-start | bytes 1572872 | tf_op jit(solution)/shard_map/ppermute | solution.py:12
  406.5 48.6 %collective-permute-start.18 = (bf16[2,512,256]{2,1,0:T(8,128)(2,1)S(1)}, bf16[2,512,256]{2,1,0:T(8,128)(2,1)S(1)}, u32[]{:S(2)}, u32[]{:S(2)}) collective-permute-start(bf16[2,512,256]{2,1,0:T(8,128)(2,1)S(1)} %pad_maximum_fusion.36), channel_id=1, source_target_pairs={{0,120},{8,128},{16,136},{24,144},{32,152},{40,160},{48,168},{56,1... | collective-permute-start | bytes 1572872 | tf_op jit(solution)/shard_map/ppermute | solution.py:12
  441.6 25.1 %collective-permute-start.23 = (bf16[2,512,256]{2,1,0:T(8,128)(2,1)S(1)}, bf16[2,512,256]{2,1,0:T(8,128)(2,1)S(1)}, u32[]{:S(2)}, u32[]{:S(2)}) collective-permute-start(bf16[2,512,256]{2,1,0:T(8,128)(2,1)S(1)} %pad_maximum_fusion.37), channel_id=1, source_target_pairs={{24,0},{32,8},{40,16},{48,24},{56,32},{64,40},{72,48},{80,56},{88,... | collective-permute-start | bytes 1572872 | tf_op jit(solution)/shard_map/ppermute | solution.py:12
  449.2 47.5 %collective-permute-start.24 = (bf16[2,512,256]{2,1,0:T(8,128)(2,1)S(1)}, bf16[2,512,256]{2,1,0:T(8,128)(2,1)S(1)}, u32[]{:S(2)}, u32[]{:S(2)}) collective-permute-start(bf16[2,512,256]{2,1,0:T(8,128)(2,1)S(1)} %pad_maximum_fusion.36), channel_id=1, source_target_pairs={{24,0},{32,8},{40,16},{48,24},{56,32},{64,40},{72,48},{80,56},{88,... | collective-permute-start | bytes 1572872 | tf_op jit(solution)/shard_map/ppermute | solution.py:12
  455.1 60.8 %collective-permute-start.22 = (bf16[2,512,256]{2,1,0:T(8,128)(2,1)S(1)}, bf16[2,512,256]{2,1,0:T(8,128)(2,1)S(1)}, u32[]{:S(2)}, u32[]{:S(2)}) collective-permute-start(bf16[2,512,256]{2,1,0:T(8,128)(2,1)S(1)} %pad_maximum_fusion.36), channel_id=1, source_target_pairs={{0,104},{8,112},{16,120},{24,128},{32,136},{40,144},{48,152},{56,1... | collective-permute-start | bytes 1572872 | tf_op jit(solution)/shard_map/ppermute | solution.py:12
  466.7 71.3 %collective-permute-start.27 = (bf16[2,512,256]{2,1,0:T(8,128)(2,1)S(1)}, bf16[2,512,256]{2,1,0:T(8,128)(2,1)S(1)}, u32[]{:S(2)}, u32[]{:S(2)}) collective-permute-start(bf16[2,512,256]{2,1,0:T(8,128)(2,1)S(1)} %pad_maximum_fusion.37), channel_id=1, source_target_pairs={{32,0},{40,8},{48,16},{56,24},{64,32},{72,40},{80,48},{88,56},{96,... | collective-permute-start | bytes 1572872 | tf_op jit(solution)/shard_map/ppermute | solution.py:12
  496.7 58.2 %collective-permute-start.28 = (bf16[2,512,256]{2,1,0:T(8,128)(2,1)S(1)}, bf16[2,512,256]{2,1,0:T(8,128)(2,1)S(1)}, u32[]{:S(2)}, u32[]{:S(2)}) collective-permute-start(bf16[2,512,256]{2,1,0:T(8,128)(2,1)S(1)} %pad_maximum_fusion.36), channel_id=1, source_target_pairs={{32,0},{40,8},{48,16},{56,24},{64,32},{72,40},{80,48},{88,56},{96,... | collective-permute-start | bytes 1572872 | tf_op jit(solution)/shard_map/ppermute | solution.py:12
  515.9 25.1 %collective-permute-start.21 = (bf16[2,512,256]{2,1,0:T(8,128)(2,1)S(1)}, bf16[2,512,256]{2,1,0:T(8,128)(2,1)S(1)}, u32[]{:S(2)}, u32[]{:S(2)}) collective-permute-start(bf16[2,512,256]{2,1,0:T(8,128)(2,1)S(1)} %pad_maximum_fusion.37), channel_id=1, source_target_pairs={{136,0},{144,8},{152,16},{160,24},{168,32},{176,40},{184,48},{192,... | collective-permute-start | bytes 1572872 | tf_op jit(solution)/shard_map/ppermute | solution.py:12
  538.0 36.0 %collective-permute-start.26 = (bf16[2,512,256]{2,1,0:T(8,128)(2,1)S(1)}, bf16[2,512,256]{2,1,0:T(8,128)(2,1)S(1)}, u32[]{:S(2)}, u32[]{:S(2)}) collective-permute-start(bf16[2,512,256]{2,1,0:T(8,128)(2,1)S(1)} %pad_maximum_fusion.36), channel_id=1, source_target_pairs={{0,96},{8,104},{16,112},{24,120},{32,128},{40,136},{48,144},{56,15... | collective-permute-start | bytes 1572872 | tf_op jit(solution)/shard_map/ppermute | solution.py:12
  541.0 16.9 %collective-permute-start.25 = (bf16[2,512,256]{2,1,0:T(8,128)(2,1)S(1)}, bf16[2,512,256]{2,1,0:T(8,128)(2,1)S(1)}, u32[]{:S(2)}, u32[]{:S(2)}) collective-permute-start(bf16[2,512,256]{2,1,0:T(8,128)(2,1)S(1)} %pad_maximum_fusion.37), channel_id=1, source_target_pairs={{152,0},{160,8},{168,16},{176,24},{184,32},{192,40},{200,48},{208,... | collective-permute-start | bytes 1572872 | tf_op jit(solution)/shard_map/ppermute | solution.py:12
  554.9 82.3 %collective-permute-start.31 = (bf16[2,512,256]{2,1,0:T(8,128)(2,1)S(1)}, bf16[2,512,256]{2,1,0:T(8,128)(2,1)S(1)}, u32[]{:S(2)}, u32[]{:S(2)}) collective-permute-start(bf16[2,512,256]{2,1,0:T(8,128)(2,1)S(1)} %pad_maximum_fusion.37), channel_id=1, source_target_pairs={{40,0},{48,8},{56,16},{64,24},{72,32},{80,40},{88,48},{96,56},{104... | collective-permute-start | bytes 1572872 | tf_op jit(solution)/shard_map/ppermute | solution.py:12
  557.9 44.7 %collective-permute-start.29 = (bf16[2,512,256]{2,1,0:T(8,128)(2,1)S(1)}, bf16[2,512,256]{2,1,0:T(8,128)(2,1)S(1)}, u32[]{:S(2)}, u32[]{:S(2)}) collective-permute-start(bf16[2,512,256]{2,1,0:T(8,128)(2,1)S(1)} %pad_maximum_fusion.37), channel_id=1, source_target_pairs={{160,0},{168,8},{176,16},{184,24},{192,32},{200,40},{208,48},{216,... | collective-permute-start | bytes 1572872 | tf_op jit(solution)/shard_map/ppermute | solution.py:12
  574.0 102.6 %collective-permute-start.32 = (bf16[2,512,256]{2,1,0:T(8,128)(2,1)S(1)}, bf16[2,512,256]{2,1,0:T(8,128)(2,1)S(1)}, u32[]{:S(2)}, u32[]{:S(2)}) collective-permute-start(bf16[2,512,256]{2,1,0:T(8,128)(2,1)S(1)} %pad_maximum_fusion.36), channel_id=1, source_target_pairs={{40,0},{48,8},{56,16},{64,24},{72,32},{80,40},{88,48},{96,56},{104... | collective-permute-start | bytes 1572872 | tf_op jit(solution)/shard_map/ppermute | solution.py:12
  602.6 97.5 %collective-permute-start.30 = (bf16[2,512,256]{2,1,0:T(8,128)(2,1)S(1)}, bf16[2,512,256]{2,1,0:T(8,128)(2,1)S(1)}, u32[]{:S(2)}, u32[]{:S(2)}) collective-permute-start(bf16[2,512,256]{2,1,0:T(8,128)(2,1)S(1)} %pad_maximum_fusion.36), channel_id=1, source_target_pairs={{0,88},{8,96},{16,104},{24,112},{32,120},{40,128},{48,136},{56,144... | collective-permute-start | bytes 1572872 | tf_op jit(solution)/shard_map/ppermute | solution.py:12
  632.3 26.6 %collective-permute-start.7 = (bf16[2,512,256]{2,1,0:T(8,128)(2,1)S(1)}, bf16[2,512,256]{2,1,0:T(8,128)(2,1)S(1)}, u32[]{:S(2)}, u32[]{:S(2)}) collective-permute-start(bf16[2,512,256]{2,1,0:T(8,128)(2,1)S(1)} %pad_maximum_fusion.37), channel_id=1, source_target_pairs={{96,0},{104,8},{112,16},{120,24},{128,32},{136,40},{144,48},{152,5... | collective-permute-start | bytes 1572872 | tf_op jit(solution)/shard_map/ppermute | solution.py:12
  635.3 68.9 %collective-permute-start.33 = (bf16[2,512,256]{2,1,0:T(8,128)(2,1)S(1)}, bf16[2,512,256]{2,1,0:T(8,128)(2,1)S(1)}, u32[]{:S(2)}, u32[]{:S(2)}) collective-permute-start(bf16[2,512,256]{2,1,0:T(8,128)(2,1)S(1)} %pad_maximum_fusion.37), channel_id=1, source_target_pairs={{168,0},{176,8},{184,16},{192,24},{200,32},{208,40},{216,48},{224,... | collective-permute-start | bytes 1572872 | tf_op jit(solution)/shard_map/ppermute | solution.py:12
  636.8 4.9 copy-start.54
  636.8 4.9 copy-start.79
  636.8 4.9 copy-start.90
  636.8 4.9 copy-start.91
  637.1 69.0 %collective-permute-start.3 = (bf16[2,512,256]{2,1,0:T(8,128)(2,1)S(1)}, bf16[2,512,256]{2,1,0:T(8,128)(2,1)S(1)}, u32[]{:S(2)}, u32[]{:S(2)}) collective-permute-start(bf16[2,512,256]{2,1,0:T(8,128)(2,1)S(1)} %pad_maximum_fusion.37), channel_id=1, source_target_pairs={{88,0},{96,8},{104,16},{112,24},{120,32},{128,40},{136,48},{144,56... | collective-permute-start | bytes 1572872 | tf_op jit(solution)/shard_map/ppermute | solution.py:12
  642.0 31.2 %copy-start.65 = (pred[1536]{0:T(1024)(128)(4,1)S(1)}, pred[1536]{0:T(1024)(128)(4,1)}, u32[]{:S(2)}) copy-start(pred[1536]{0:T(1024)(128)(4,1)} %get-tuple-element.273) | copy-start | bytes 4612
  642.0 31.2 %copy-start.66 = (pred[1536]{0:T(1024)(128)(4,1)S(1)}, pred[1536]{0:T(1024)(128)(4,1)}, u32[]{:S(2)}) copy-start(pred[1536]{0:T(1024)(128)(4,1)} %get-tuple-element.275) | copy-start | bytes 4612
  642.1 31.2 %copy-start.76 = (pred[1536]{0:T(1024)(128)(4,1)S(1)}, pred[1536]{0:T(1024)(128)(4,1)}, u32[]{:S(2)}) copy-start(pred[1536]{0:T(1024)(128)(4,1)} %get-tuple-element.278) | copy-start | bytes 4612
  642.1 31.2 %copy-start.77 = (pred[1536]{0:T(1024)(128)(4,1)S(1)}, pred[1536]{0:T(1024)(128)(4,1)}, u32[]{:S(2)}) copy-start(pred[1536]{0:T(1024)(128)(4,1)} %get-tuple-element.276) | copy-start | bytes 4612
  642.1 31.2 %copy-start.78 = (pred[1536]{0:T(1024)(128)(4,1)S(1)}, pred[1536]{0:T(1024)(128)(4,1)}, u32[]{:S(2)}) copy-start(pred[1536]{0:T(1024)(128)(4,1)} %get-tuple-element.274) | copy-start | bytes 4612
  642.1 31.2 %copy-start.88 = (pred[64]{0:T(512)(128)(4,1)S(1)}, pred[64]{0:T(512)(128)(4,1)}, u32[]{:S(2)}) copy-start(pred[64]{0:T(512)(128)(4,1)} %get-tuple-element.292) | copy-start | bytes 196
  642.1 31.2 %copy-start.89 = (s32[64]{0:T(128)S(1)}, s32[64]{0:T(128)}, u32[]{:S(2)}) copy-start(s32[64]{0:T(128)} %get-tuple-element.286) | copy-start | bytes 772
  658.9 49.4 %collective-permute-start.15 = (bf16[2,512,256]{2,1,0:T(8,128)(2,1)S(1)}, bf16[2,512,256]{2,1,0:T(8,128)(2,1)S(1)}, u32[]{:S(2)}, u32[]{:S(2)}) collective-permute-start(bf16[2,512,256]{2,1,0:T(8,128)(2,1)S(1)} %pad_maximum_fusion.37), channel_id=1, source_target_pairs={{120,0},{128,8},{136,16},{144,24},{152,32},{160,40},{168,48},{176,... | collective-permute-start | bytes 1572872 | tf_op jit(solution)/shard_map/ppermute | solution.py:12
  676.7 36.3 %collective-permute-start.17 = (bf16[2,512,256]{2,1,0:T(8,128)(2,1)S(1)}, bf16[2,512,256]{2,1,0:T(8,128)(2,1)S(1)}, u32[]{:S(2)}, u32[]{:S(2)}) collective-permute-start(bf16[2,512,256]{2,1,0:T(8,128)(2,1)S(1)} %pad_maximum_fusion.37), channel_id=1, source_target_pairs={{128,0},{136,8},{144,16},{152,24},{160,32},{168,40},{176,48},{184,... | collective-permute-start | bytes 1572872 | tf_op jit(solution)/shard_map/ppermute | solution.py:12
  700.1 18.0 %collective-permute-start.11 = (bf16[2,512,256]{2,1,0:T(8,128)(2,1)S(1)}, bf16[2,512,256]{2,1,0:T(8,128)(2,1)S(1)}, u32[]{:S(2)}, u32[]{:S(2)}) collective-permute-start(bf16[2,512,256]{2,1,0:T(8,128)(2,1)S(1)} %pad_maximum_fusion.37), channel_id=1, source_target_pairs={{104,0},{112,8},{120,16},{128,24},{136,32},{144,40},{152,48},{160,... | collective-permute-start | bytes 1572872 | tf_op jit(solution)/shard_map/ppermute | solution.py:12
  714.8 4.0 copy-start.63
  714.8 4.0 copy-start.64
  753.3 72.7 %copy-start.2 = (bf16[512,4,256]{2,0,1:T(8,128)(2,1)S(1)}, bf16[512,4,256]{2,0,1:T(8,128)(2,1)}, u32[]{:S(2)}) copy-start(bf16[512,4,256]{2,0,1:T(8,128)(2,1)} %all-gather.3.cloned.1.call-done) | copy-start | bytes 3145732
  753.3 72.7 %copy-start.33 = (bf16[128,256]{1,0:T(8,128)(2,1)S(1)}, bf16[128,256]{1,0:T(8,128)(2,1)}, u32[]{:S(2)}) copy-start(bf16[128,256]{1,0:T(8,128)(2,1)} %param.8) | copy-start | bytes 196612
  753.3 294.1 %all-reduce.6.cloned.1.call-start = ((), (), s32[]{:S(2)}) async-start(), calls=%async_computation.5 | async-start | bytes 524288 | tf_op jit(solution)/shard_map/psum | solution.py:179
  827.8 476.0 %all-reduce.4.cloned.1.call-start = ((), (), s32[]{:S(2)}) async-start(), calls=%async_computation.4 | async-start | bytes 524288 | tf_op jit(solution)/shard_map/psum | solution.py:180
  (70 other events, 100.3 us)
Sparse Core Ops, SparseCore 0:
  11.2 53.4 all-gather.2
  72.7 82.5 reduce-scatter.1
  753.4 70.0 all-gather.4
  827.9 219.4 all-reduce.5
  1054.1 249.5 all-reduce.3
where the time goes:
time: 1330 us; the launch traced here: 1320 us
  waiting for transfers between devices  724 us (54%)
  starting transfers between devices  251 us (19%)
  blocking collectives  146 us (11%)
  other arithmetic  67.6 us (5%)
  matrix products  53.3 us (4%)
  local copies, waits for them, and re-layouts  42.2 us (3%)
  between operations  29.7 us (2%)
    psum x1, waiting for transfers between devices, local(): lax.psum((bilinear_part, loss_sum), ('tile', 'mlp'))  255 us
    ppermute x34, starting transfers between devices, shifted(): return lax.ppermute(array, axis, pairs)  251 us
    ppermute x34, waiting for transfers between devices, shifted(): return lax.ppermute(array, axis, pairs)  198 us
    psum x1, waiting for transfers between devices, local(): grad_in, grad_out = lax.psum((in_part, out_part), 'tile')  132 us
    psum x1, blocking collectives, local(): lax.psum((bilinear_part, loss_sum), ('tile', 'mlp'))  75.1 us
    reduce_scatter x1, waiting for transfers between devices, local(): lax.psum_scatter(jnp.einsum('rch,hf->rcf', active, w_out, preferred_eleme...  70.2 us
    all_gather x1, waiting for transfers between devices, local(): embed_whole = lax.all_gather(embed_grad, 'mlp', axis=0, tiled=True)  70.2 us
    all_gather x1, blocking collectives, local(): lax.all_gather(post_local, 'mlp', axis=0, tiled=True)  35.8 us
  transfers between devices with their start and end apart: 39, of which 16 were waited for; matrix products, arithmetic and copies ran while one was open for 9% of the time, Pallas kernels for 0%

commit v1 on v0

--- a/solution.py
+++ b/solution.py
@@ -177,7 +177,7 @@
     in_part = jnp.einsum("rcf,rch->fh", whole_x, hidden_grad, preferred_element_type=jnp.float32)
     out_part = jnp.einsum("rch,rcf->hf", active, embed_whole, preferred_element_type=jnp.float32)
     grad_in, grad_out = lax.psum((in_part, out_part), "tile")
-    grad_bilinear, loss_total = lax.psum((bilinear_part, loss_sum), ("tile", "mlp"))
+    grad_bilinear, loss_total = lax.psum(lax.psum((bilinear_part, loss_sum), "mlp"), "tile")
     pair_loss = loss_total / (2.0 * tile_count * site_rows * 27 * site_rows)
     return (pair_loss, grad_in, grad_out, grad_bilinear)
 

time: 1330 us -> 1180 us (0.89)
  waiting for transfers between devices: 724 us -> 548 us
  starting transfers between devices: 251 us -> 275 us
    psum x1, waiting for transfers between devices: 255 us -> 86.1 us  [local(): lax.psum((bilinear_part, loss_sum), 'mlp')]
    ppermute x34, starting transfers between devices: 251 us -> 275 us  [shifted(): return lax.ppermute(array, axis, pairs)]
    ppermute x34, waiting for transfers between devices: 198 us -> 182 us  [shifted(): return lax.ppermute(array, axis, pairs)]
    psum x1 -> x2, blocking collectives: 75.1 us -> 75.4 us  [the longest x1 53.6 us: local(): lax.psum(lax.psum((bilinear_part, loss_sum), 'mlp'), 'tile')]
  transfers between devices with their start and end apart: 39 -> 39, of which waited for: 16 -> 15; matrix products, arithmetic and copies ran while one was open for 9% -> 10% of each run, Pallas kernels for 0% -> 0%
where the time goes in v1:
time: 1180 us; the launch traced here: 1160 us
  waiting for transfers between devices  548 us (46%)
  starting transfers between devices  275 us (23%)
  blocking collectives  147 us (12%)
  other arithmetic  67.9 us (6%)
  matrix products  56 us (5%)
  local copies, waits for them, and re-layouts  41.6 us (4%)
  between operations  29.5 us (2%)
    ppermute x34, starting transfers between devices, shifted(): return lax.ppermute(array, axis, pairs)  275 us
    ppermute x34, waiting for transfers between devices, shifted(): return lax.ppermute(array, axis, pairs)  182 us
    psum x1, waiting for transfers between devices, local(): grad_in, grad_out = lax.psum((in_part, out_part), 'tile')  137 us
    psum x1, waiting for transfers between devices, local(): lax.psum((bilinear_part, loss_sum), 'mlp')  86.1 us
    all_gather x1, waiting for transfers between devices, local(): embed_whole = lax.all_gather(embed_grad, 'mlp', axis=0, tiled=True)  72.4 us
    reduce_scatter x1, waiting for transfers between devices, local(): lax.psum_scatter(jnp.einsum('rch,hf->rcf', active, w_out, preferred_eleme...  70.1 us
    psum x1, blocking collectives, local(): lax.psum(lax.psum((bilinear_part, loss_sum), 'mlp'), 'tile')  53.6 us
    all_gather x1, blocking collectives, local(): lax.all_gather(post_local, 'mlp', axis=0, tiled=True)  35.9 us
  transfers between devices with their start and end apart: 39, of which 15 were waited for; matrix products, arithmetic and copies ran while one was open for 10% of the time, Pallas kernels for 0%

profile of v1, /device:TPU:2, one launch (start us, length us, event | category | flops | bytes accessed | tf_op | source)
XLA Modules:
  0.0 1164.8 jit_solution(15656909752436222987)
XLA Ops:
  7.2 1.6 copy.14
  9.6 2.7 constant_dynamic-slice_fusion.65
  32.4 1.8 constant_dynamic-slice_fusion.77
  69.4 1.6 fusion.714
  71.0 1.8 fusion.712
  85.4 70.1 %reduce-scatter.2.cloned.1.call-done = f32[64,4,256]{2,0,1:T(8,128)} async-done(((f32[512,4,256]{2,0,1:T(8,128)}), f32[64,4,256]{2,0,1:T(8,128)}) %reduce-scatter.2.cloned.1.call-update) | async-done | bytes 262160 | tf_op jit(solution)/shard_map/reduce_scatter | solution.py:53
  156.6 35.9 %all_gather.13 = bf16[512,2,256]{2,0,1:T(8,128)(2,1)S(1)} all-gather(bf16[64,2,256]{2,0,1:T(8,128)(2,1)S(1)} %slice.1000), channel_id=1, replica_groups=mesh['tile'=32,'mlp'=8] {'mlp'}, dimensions={0}, use_global_device_ids=true | all-gather | bytes 589824 | tf_op jit(solution)/shard_map/all_gather | solution.py:75
  192.7 35.5 %all_gather.14 = bf16[512,2,256]{2,0,1:T(8,128)(2,1)S(1)} all-gather(bf16[64,2,256]{2,0,1:T(8,128)(2,1)S(1)} %convolution_convert_fusion.1), channel_id=1, replica_groups=mesh['tile'=32,'mlp'=8] {'mlp'}, dimensions={0}, use_global_device_ids=true | all-gather | bytes 589824 | tf_op jit(solution)/shard_map/all_gather | solution.py:76
  228.4 4.9 collective-permute-start.5
  233.9 5.1 collective-permute-start.6
  241.6 1.9 collective-permute-start.1
  243.5 3.1 collective-permute-start.2
  246.6 10.0 collective-permute-done.5
  257.3 32.7 %collective-permute-done.6 = bf16[2,512,256]{2,1,0:T(8,128)(2,1)S(1)} collective-permute-done((bf16[2,512,256]{2,1,0:T(8,128)(2,1)S(1)}, bf16[2,512,256]{2,1,0:T(8,128)(2,1)S(1)}, u32[]{:S(2)}, u32[]{:S(2)}) %collective-permute-start.6) | collective-permute-done | bytes 524320 | tf_op jit(solution)/shard_map/ppermute | solution.py:12
  290.0 5.0 collective-permute-start.9
  295.0 9.2 collective-permute-start.10
  305.1 27.2 %collective-permute-done.2 = bf16[2,512,256]{2,1,0:T(8,128)(2,1)S(1)} collective-permute-done((bf16[2,512,256]{2,1,0:T(8,128)(2,1)S(1)}, bf16[2,512,256]{2,1,0:T(8,128)(2,1)S(1)}, u32[]{:S(2)}, u32[]{:S(2)}) %collective-permute-start.2) | collective-permute-done | bytes 524320 | tf_op jit(solution)/shard_map/ppermute | solution.py:12
  332.2 13.8 %collective-permute-start.13 = (bf16[2,512,256]{2,1,0:T(8,128)(2,1)S(1)}, bf16[2,512,256]{2,1,0:T(8,128)(2,1)S(1)}, u32[]{:S(2)}, u32[]{:S(2)}) collective-permute-start(bf16[2,512,256]{2,1,0:T(8,128)(2,1)S(1)} %pad_maximum_fusion.37), channel_id=1, source_target_pairs={{0,8},{8,16},{16,24},{24,32},{32,40},{40,48},{48,56},{56,64},{64,7... | collective-permute-start | bytes 1572872 | tf_op jit(solution)/shard_map/ppermute | solution.py:12
  346.1 1.9 collective-permute-start.14
  349.5 13.4 %collective-permute-done.10 = bf16[2,512,256]{2,1,0:T(8,128)(2,1)S(1)} collective-permute-done((bf16[2,512,256]{2,1,0:T(8,128)(2,1)S(1)}, bf16[2,512,256]{2,1,0:T(8,128)(2,1)S(1)}, u32[]{:S(2)}, u32[]{:S(2)}) %collective-permute-start.10) | collective-permute-done | bytes 524320 | tf_op jit(solution)/shard_map/ppermute | solution.py:12
  365.0 37.0 %collective-permute-start.19 = (bf16[2,512,256]{2,1,0:T(8,128)(2,1)S(1)}, bf16[2,512,256]{2,1,0:T(8,128)(2,1)S(1)}, u32[]{:S(2)}, u32[]{:S(2)}) collective-permute-start(bf16[2,512,256]{2,1,0:T(8,128)(2,1)S(1)} %pad_maximum_fusion.37), channel_id=1, source_target_pairs={{8,0},{16,8},{24,16},{32,24},{40,32},{48,40},{56,48},{64,56},{72,6... | collective-permute-start | bytes 1572872 | tf_op jit(solution)/shard_map/ppermute | solution.py:12
  402.8 43.8 %collective-permute-start.20 = (bf16[2,512,256]{2,1,0:T(8,128)(2,1)S(1)}, bf16[2,512,256]{2,1,0:T(8,128)(2,1)S(1)}, u32[]{:S(2)}, u32[]{:S(2)}) collective-permute-start(bf16[2,512,256]{2,1,0:T(8,128)(2,1)S(1)} %pad_maximum_fusion.36), channel_id=1, source_target_pairs={{8,0},{16,8},{24,16},{32,24},{40,32},{48,40},{56,48},{64,56},{72,6... | collective-permute-start | bytes 1572872 | tf_op jit(solution)/shard_map/ppermute | solution.py:12
  447.4 6.1 collective-permute-start.18
  454.3 4.0 collective-permute-start.23
  459.0 3.5 collective-permute-start.24
  463.5 6.5 collective-permute-start.22
  470.7 8.4 collective-permute-done.23
  479.1 8.0 collective-permute-start.27
  487.9 24.7 %collective-permute-done.24 = bf16[2,512,256]{2,1,0:T(8,128)(2,1)S(1)} collective-permute-done((bf16[2,512,256]{2,1,0:T(8,128)(2,1)S(1)}, bf16[2,512,256]{2,1,0:T(8,128)(2,1)S(1)}, u32[]{:S(2)}, u32[]{:S(2)}) %collective-permute-start.24) | collective-permute-done | bytes 524320 | tf_op jit(solution)/shard_map/ppermute | solution.py:12
  512.6 24.1 %collective-permute-start.28 = (bf16[2,512,256]{2,1,0:T(8,128)(2,1)S(1)}, bf16[2,512,256]{2,1,0:T(8,128)(2,1)S(1)}, u32[]{:S(2)}, u32[]{:S(2)}) collective-permute-start(bf16[2,512,256]{2,1,0:T(8,128)(2,1)S(1)} %pad_maximum_fusion.36), channel_id=1, source_target_pairs={{32,0},{40,8},{48,16},{56,24},{64,32},{72,40},{80,48},{88,56},{96,... | collective-permute-start | bytes 1572872 | tf_op jit(solution)/shard_map/ppermute | solution.py:12
  538.8 12.6 %collective-permute-done.27 = bf16[2,512,256]{2,1,0:T(8,128)(2,1)S(1)} collective-permute-done((bf16[2,512,256]{2,1,0:T(8,128)(2,1)S(1)}, bf16[2,512,256]{2,1,0:T(8,128)(2,1)S(1)}, u32[]{:S(2)}, u32[]{:S(2)}) %collective-permute-start.27) | collective-permute-done | bytes 524320 | tf_op jit(solution)/shard_map/ppermute | solution.py:12
  551.4 1.9 collective-permute-start.26
  556.2 12.1 %collective-permute-done.28 = bf16[2,512,256]{2,1,0:T(8,128)(2,1)S(1)} collective-permute-done((bf16[2,512,256]{2,1,0:T(8,128)(2,1)S(1)}, bf16[2,512,256]{2,1,0:T(8,128)(2,1)S(1)}, u32[]{:S(2)}, u32[]{:S(2)}) %collective-permute-start.28) | collective-permute-done | bytes 524320 | tf_op jit(solution)/shard_map/ppermute | solution.py:12
  568.4 1.9 collective-permute-start.31
  573.2 13.2 %collective-permute-done.26 = bf16[2,512,256]{2,1,0:T(8,128)(2,1)S(1)} collective-permute-done((bf16[2,512,256]{2,1,0:T(8,128)(2,1)S(1)}, bf16[2,512,256]{2,1,0:T(8,128)(2,1)S(1)}, u32[]{:S(2)}, u32[]{:S(2)}) %collective-permute-start.26) | collective-permute-done | bytes 524320 | tf_op jit(solution)/shard_map/ppermute | solution.py:12
  586.4 1.9 collective-permute-start.32
  589.4 54.6 %collective-permute-start.30 = (bf16[2,512,256]{2,1,0:T(8,128)(2,1)S(1)}, bf16[2,512,256]{2,1,0:T(8,128)(2,1)S(1)}, u32[]{:S(2)}, u32[]{:S(2)}) collective-permute-start(bf16[2,512,256]{2,1,0:T(8,128)(2,1)S(1)} %pad_maximum_fusion.36), channel_id=1, source_target_pairs={{0,88},{8,96},{16,104},{24,112},{32,120},{40,128},{48,136},{56,144... | collective-permute-start | bytes 1572872 | tf_op jit(solution)/shard_map/ppermute | solution.py:12
  645.1 1.9 collective-permute-start.7
  650.0 1.9 collective-permute-start.3
  653.1 27.9 %collective-permute-done.7 = bf16[2,512,256]{2,1,0:T(8,128)(2,1)S(1)} collective-permute-done((bf16[2,512,256]{2,1,0:T(8,128)(2,1)S(1)}, bf16[2,512,256]{2,1,0:T(8,128)(2,1)S(1)}, u32[]{:S(2)}, u32[]{:S(2)}) %collective-permute-start.7) | collective-permute-done | bytes 524320 | tf_op jit(solution)/shard_map/ppermute | solution.py:12
  681.0 13.2 %collective-permute-start.15 = (bf16[2,512,256]{2,1,0:T(8,128)(2,1)S(1)}, bf16[2,512,256]{2,1,0:T(8,128)(2,1)S(1)}, u32[]{:S(2)}, u32[]{:S(2)}) collective-permute-start(bf16[2,512,256]{2,1,0:T(8,128)(2,1)S(1)} %pad_maximum_fusion.37), channel_id=1, source_target_pairs={{120,0},{128,8},{136,16},{144,24},{152,32},{160,40},{168,48},{176,... | collective-permute-start | bytes 1572872 | tf_op jit(solution)/shard_map/ppermute | solution.py:12
  695.4 3.4 fusion.103
  698.8 2.1 collective-permute-start.17
  703.1 10.7 collective-permute-start.11
  721.2 3.4 fusion.97
  727.7 3.5 fusion.109
  735.0 1.9 fusion.365
  737.0 2.5 fusion.364
  739.5 2.1 convolution_add_fusion.15
  741.5 2.3 convolution_add_fusion.7
  743.9 2.1 convolution_add_fusion.14
  746.1 2.2 convolution_add_fusion.6
  748.3 2.1 convolution_add_fusion.13
  760.9 1.5 fusion.76
  764.1 72.4 %all-gather.5.cloned.1.call-done = bf16[512,4,256]{2,0,1:T(8,128)(2,1)} async-done(((bf16[64,4,256]{2,0,1:T(8,128)(2,1)}), bf16[512,4,256]{2,0,1:T(8,128)(2,1)}) %all-gather.5.cloned.1.call-update) | async-done | bytes 1048592 | tf_op jit(solution)/shard_map/all_gather | solution.py:173
  836.5 2.9 convolution_bitcast_fusion.2
  839.5 2.4 convolution_bitcast_fusion.1
  841.9 86.1 %all-reduce.4.cloned.1.call-done = f32[256,256]{1,0:T(8,128)} async-done(((f32[256,256]{1,0:T(8,128)}), f32[256,256]{1,0:T(8,128)}) %all-reduce.4.cloned.1.call-update) | async-done | bytes 262160 | tf_op jit(solution)/shard_map/psum | solution.py:180
  939.1 21.7 %psum.42 = f32[]{:T(128)} all-reduce(f32[]{:T(128)S(6)} %add.980), channel_id=1, replica_groups=mesh['tile'=32,'mlp'=8] {'mlp'}, use_global_device_ids=true, to_apply=%region_19.20 | all-reduce | flops 1 | bytes 8 | tf_op jit(solution)/shard_map/psum | solution.py:180
  960.8 53.6 %psum.43 = f32[]{:T(128)} all-reduce(f32[]{:T(128)} %psum.42), channel_id=1, replica_groups=mesh['tile'=32,'mlp'=8] {'tile'}, use_global_device_ids=true, to_apply=%region_20.21 | all-reduce | flops 1 | bytes 8 | tf_op jit(solution)/shard_map/psum | solution.py:180
  1015.1 136.8 %all-reduce.6.cloned.1.call-done = (f32[256,128]{0,1:T(8,128)}, f32[128,256]{1,0:T(8,128)}, f32[256,256]{1,0:T(8,128)}) async-done(((f32[256,128]{0,1:T(8,128)}, f32[128,256]{1,0:T(8,128)}, f32[256,256]{1,0:T(8,128)}), (f32[256,128]{0,1:T(8,128)}, f32[128,256]{1,0:T(8,128)}, f32[256,256]{1,0:T(8,128)})) %all-reduce.6.cloned.1.call-update) | async-done | bytes 524304 | tf_op jit(solution)/shard_map/psum | solution.py:179
  1151.9 1.7 copy.17
  1153.5 1.6 copy.24
  1155.1 1.7 copy.25
  (429 shorter events, 126.0 us)
Async XLA Ops:
  7.2 185.4 %copy-start = (bf16[256,256]{1,0:T(8,128)(2,1)S(1)}, bf16[256,256]{1,0:T(8,128)(2,1)}, u32[]{:S(2)}) copy-start(bf16[256,256]{1,0:T(8,128)(2,1)} %param.9) | copy-start | bytes 393220
  7.2 62.2 %copy-start.31 = (bf16[256,128]{1,0:T(8,128)(2,1)S(1)}, bf16[256,128]{1,0:T(8,128)(2,1)}, u32[]{:S(2)}) copy-start(bf16[256,128]{1,0:T(8,128)(2,1)} %param.7) | copy-start | bytes 196612
  7.2 62.2 %all-gather.3.cloned.1.call-start = ((), (), s32[]{:S(2)}) async-start(), calls=%async_computation.1 | async-start | bytes 1179648 | tf_op jit(solution)/shard_map/all_gather | solution.py:50
  8.9 146.7 %reduce-scatter.2.cloned.1.call-start = ((), (), s32[]{:S(2)}) async-start(), calls=%async_computation.2 | async-start | bytes 2359296 | tf_op jit(solution)/shard_map/reduce_scatter | solution.py:53
  9.2 61.8 %copy-start.32 = (bf16[128,256]{1,0:T(8,128)(2,1)S(1)}, bf16[128,256]{1,0:T(8,128)(2,1)}, u32[]{:S(2)}) copy-start(bf16[128,256]{1,0:T(8,128)(2,1)} %param.8) | copy-start | bytes 196612
  72.8 82.7 %copy-start.1 = (bf16[1,64,2,2,256]{4,1,3,2,0:T(8,128)(2,1)S(1)}, bf16[1,64,2,2,256]{4,1,3,2,0:T(8,128)(2,1)}, u32[]{:S(2)}) copy-start(bf16[1,64,2,2,256]{4,1,3,2,0:T(8,128)(2,1)} %copy.14) | copy-start | bytes 393220
  72.9 763.6 %all-gather.5.cloned.1.call-start = ((), (), s32[]{:S(2)}) async-start(), calls=%async_computation.3 | async-start | bytes 1179648 | tf_op jit(solution)/shard_map/all_gather | solution.py:173
  72.9 119.6 %copy-start.84 = (s32[64]{0:T(128)}, s32[64]{0:T(128)S(1)}, u32[]{:S(2)}) copy-start(s32[64]{0:T(128)S(1)} %iota_add_fusion.26) | copy-start | bytes 772
  73.6 647.6 %copy-start.51 = (s32[1536]{0:T(1024)}, s32[1536]{0:T(1024)S(1)}, u32[]{:S(2)}) copy-start(s32[1536]{0:T(1024)S(1)} %pad_add_fusion) | copy-start | bytes 18436
  73.6 641.3 %copy-start.45 = (s32[1536]{0:T(1024)}, s32[1536]{0:T(1024)S(1)}, u32[]{:S(2)}) copy-start(s32[1536]{0:T(1024)S(1)} %pad_add_fusion.2) | copy-start | bytes 18436
  73.6 641.7 %copy-start.43 = (s32[1536]{0:T(1024)}, s32[1536]{0:T(1024)S(1)}, u32[]{:S(2)}) copy-start(s32[1536]{0:T(1024)S(1)} %pad_add_fusion.3) | copy-start | bytes 18436
  73.6 643.4 %copy-start.41 = (s32[1536]{0:T(1024)}, s32[1536]{0:T(1024)S(1)}, u32[]{:S(2)}) copy-start(s32[1536]{0:T(1024)S(1)} %pad_add_fusion.4) | copy-start | bytes 18436
  73.8 652.0 %copy-start.37 = (s32[1536]{0:T(1024)}, s32[1536]{0:T(1024)S(1)}, u32[]{:S(2)}) copy-start(s32[1536]{0:T(1024)S(1)} %pad_add_fusion.8) | copy-start | bytes 18436
  228.4 28.2 %collective-permute-start.5 = (bf16[2,512,256]{2,1,0:T(8,128)(2,1)S(1)}, bf16[2,512,256]{2,1,0:T(8,128)(2,1)S(1)}, u32[]{:S(2)}, u32[]{:S(2)}) collective-permute-start(bf16[2,512,256]{2,1,0:T(8,128)(2,1)S(1)} %pad_maximum_fusion.37), channel_id=1, source_target_pairs={{0,32},{8,40},{16,48},{24,56},{32,64},{40,72},{48,80},{56,88},{64,... | collective-permute-start | bytes 1572872 | tf_op jit(solution)/shard_map/ppermute | solution.py:12
  233.9 56.1 %collective-permute-start.6 = (bf16[2,512,256]{2,1,0:T(8,128)(2,1)S(1)}, bf16[2,512,256]{2,1,0:T(8,128)(2,1)S(1)}, u32[]{:S(2)}, u32[]{:S(2)}) collective-permute-start(bf16[2,512,256]{2,1,0:T(8,128)(2,1)S(1)} %pad_maximum_fusion.36), channel_id=1, source_target_pairs={{0,32},{8,40},{16,48},{24,56},{32,64},{40,72},{48,80},{56,88},{64,... | collective-permute-start | bytes 1572872 | tf_op jit(solution)/shard_map/ppermute | solution.py:12
  240.3 54.7 %collective-permute-start.4 = (bf16[2,512,256]{2,1,0:T(8,128)(2,1)S(1)}, bf16[2,512,256]{2,1,0:T(8,128)(2,1)S(1)}, u32[]{:S(2)}, u32[]{:S(2)}) collective-permute-start(bf16[2,512,256]{2,1,0:T(8,128)(2,1)S(1)} %pad_maximum_fusion.36), channel_id=1, source_target_pairs={{0,160},{8,168},{16,176},{24,184},{32,192},{40,200},{48,208},{56,2... | collective-permute-start | bytes 1572872 | tf_op jit(solution)/shard_map/ppermute | solution.py:12
  241.6 62.7 %collective-permute-start.1 = (bf16[2,512,256]{2,1,0:T(8,128)(2,1)S(1)}, bf16[2,512,256]{2,1,0:T(8,128)(2,1)S(1)}, u32[]{:S(2)}, u32[]{:S(2)}) collective-permute-start(bf16[2,512,256]{2,1,0:T(8,128)(2,1)S(1)} %pad_maximum_fusion.37), channel_id=1, source_target_pairs={{0,40},{8,48},{16,56},{24,64},{32,72},{40,80},{48,88},{56,96},{64,... | collective-permute-start | bytes 1572872 | tf_op jit(solution)/shard_map/ppermute | solution.py:12
  243.5 88.7 %collective-permute-start.2 = (bf16[2,512,256]{2,1,0:T(8,128)(2,1)S(1)}, bf16[2,512,256]{2,1,0:T(8,128)(2,1)S(1)}, u32[]{:S(2)}, u32[]{:S(2)}) collective-permute-start(bf16[2,512,256]{2,1,0:T(8,128)(2,1)S(1)} %pad_maximum_fusion.36), channel_id=1, source_target_pairs={{0,40},{8,48},{16,56},{24,64},{32,72},{40,80},{48,88},{56,96},{64,... | collective-permute-start | bytes 1572872 | tf_op jit(solution)/shard_map/ppermute | solution.py:12
  256.6 89.5 %collective-permute-start = (bf16[2,512,256]{2,1,0:T(8,128)(2,1)S(1)}, bf16[2,512,256]{2,1,0:T(8,128)(2,1)S(1)}, u32[]{:S(2)}, u32[]{:S(2)}) collective-permute-start(bf16[2,512,256]{2,1,0:T(8,128)(2,1)S(1)} %pad_maximum_fusion.36), channel_id=1, source_target_pairs={{0,168},{8,176},{16,184},{24,192},{32,200},{40,208},{48,216},{56,2... | collective-permute-start | bytes 1572872 | tf_op jit(solution)/shard_map/ppermute | solution.py:12
  290.0 58.8 %collective-permute-start.9 = (bf16[2,512,256]{2,1,0:T(8,128)(2,1)S(1)}, bf16[2,512,256]{2,1,0:T(8,128)(2,1)S(1)}, u32[]{:S(2)}, u32[]{:S(2)}) collective-permute-start(bf16[2,512,256]{2,1,0:T(8,128)(2,1)S(1)} %pad_maximum_fusion.37), channel_id=1, source_target_pairs={{0,24},{8,32},{16,40},{24,48},{32,56},{40,64},{48,72},{56,80},{64,... | collective-permute-start | bytes 1572872 | tf_op jit(solution)/shard_map/ppermute | solution.py:12
  295.0 67.9 %collective-permute-start.10 = (bf16[2,512,256]{2,1,0:T(8,128)(2,1)S(1)}, bf16[2,512,256]{2,1,0:T(8,128)(2,1)S(1)}, u32[]{:S(2)}, u32[]{:S(2)}) collective-permute-start(bf16[2,512,256]{2,1,0:T(8,128)(2,1)S(1)} %pad_maximum_fusion.36), channel_id=1, source_target_pairs={{0,24},{8,32},{16,40},{24,48},{32,56},{40,64},{48,72},{56,80},{64,... | collective-permute-start | bytes 1572872 | tf_op jit(solution)/shard_map/ppermute | solution.py:12
  304.3 60.7 %collective-permute-start.8 = (bf16[2,512,256]{2,1,0:T(8,128)(2,1)S(1)}, bf16[2,512,256]{2,1,0:T(8,128)(2,1)S(1)}, u32[]{:S(2)}, u32[]{:S(2)}) collective-permute-start(bf16[2,512,256]{2,1,0:T(8,128)(2,1)S(1)} %pad_maximum_fusion.36), channel_id=1, source_target_pairs={{0,152},{8,160},{16,168},{24,176},{32,184},{40,192},{48,200},{56,2... | collective-permute-start | bytes 1572872 | tf_op jit(solution)/shard_map/ppermute | solution.py:12
  332.2 70.5 %collective-permute-start.13 = (bf16[2,512,256]{2,1,0:T(8,128)(2,1)S(1)}, bf16[2,512,256]{2,1,0:T(8,128)(2,1)S(1)}, u32[]{:S(2)}, u32[]{:S(2)}) collective-permute-start(bf16[2,512,256]{2,1,0:T(8,128)(2,1)S(1)} %pad_maximum_fusion.37), channel_id=1, source_target_pairs={{0,8},{8,16},{16,24},{24,32},{32,40},{40,48},{48,56},{56,64},{64,7... | collective-permute-start | bytes 1572872 | tf_op jit(solution)/shard_map/ppermute | solution.py:12
  346.1 101.2 %collective-permute-start.14 = (bf16[2,512,256]{2,1,0:T(8,128)(2,1)S(1)}, bf16[2,512,256]{2,1,0:T(8,128)(2,1)S(1)}, u32[]{:S(2)}, u32[]{:S(2)}) collective-permute-start(bf16[2,512,256]{2,1,0:T(8,128)(2,1)S(1)} %pad_maximum_fusion.36), channel_id=1, source_target_pairs={{0,8},{8,16},{16,24},{24,32},{32,40},{40,48},{48,56},{56,64},{64,7... | collective-permute-start | bytes 1572872 | tf_op jit(solution)/shard_map/ppermute | solution.py:12
  348.8 296.3 %collective-permute-start.12 = (bf16[2,512,256]{2,1,0:T(8,128)(2,1)S(1)}, bf16[2,512,256]{2,1,0:T(8,128)(2,1)S(1)}, u32[]{:S(2)}, u32[]{:S(2)}) collective-permute-start(bf16[2,512,256]{2,1,0:T(8,128)(2,1)S(1)} %pad_maximum_fusion.36), channel_id=1, source_target_pairs={{0,136},{8,144},{16,152},{24,160},{32,168},{40,176},{48,184},{56,1... | collective-permute-start | bytes 1572872 | tf_op jit(solution)/shard_map/ppermute | solution.py:12
  363.0 285.2 %collective-permute-start.16 = (bf16[2,512,256]{2,1,0:T(8,128)(2,1)S(1)}, bf16[2,512,256]{2,1,0:T(8,128)(2,1)S(1)}, u32[]{:S(2)}, u32[]{:S(2)}) collective-permute-start(bf16[2,512,256]{2,1,0:T(8,128)(2,1)S(1)} %pad_maximum_fusion.36), channel_id=1, source_target_pairs={{0,128},{8,136},{16,144},{24,152},{32,160},{40,168},{48,176},{56,1... | collective-permute-start | bytes 1572872 | tf_op jit(solution)/shard_map/ppermute | solution.py:12
  365.0 89.3 %collective-permute-start.19 = (bf16[2,512,256]{2,1,0:T(8,128)(2,1)S(1)}, bf16[2,512,256]{2,1,0:T(8,128)(2,1)S(1)}, u32[]{:S(2)}, u32[]{:S(2)}) collective-permute-start(bf16[2,512,256]{2,1,0:T(8,128)(2,1)S(1)} %pad_maximum_fusion.37), channel_id=1, source_target_pairs={{8,0},{16,8},{24,16},{32,24},{40,32},{48,40},{56,48},{64,56},{72,6... | collective-permute-start | bytes 1572872 | tf_op jit(solution)/shard_map/ppermute | solution.py:12
  402.8 56.2 %collective-permute-start.20 = (bf16[2,512,256]{2,1,0:T(8,128)(2,1)S(1)}, bf16[2,512,256]{2,1,0:T(8,128)(2,1)S(1)}, u32[]{:S(2)}, u32[]{:S(2)}) collective-permute-start(bf16[2,512,256]{2,1,0:T(8,128)(2,1)S(1)} %pad_maximum_fusion.36), channel_id=1, source_target_pairs={{8,0},{16,8},{24,16},{32,24},{40,32},{48,40},{56,48},{64,56},{72,6... | collective-permute-start | bytes 1572872 | tf_op jit(solution)/shard_map/ppermute | solution.py:12
  447.4 16.1 %collective-permute-start.18 = (bf16[2,512,256]{2,1,0:T(8,128)(2,1)S(1)}, bf16[2,512,256]{2,1,0:T(8,128)(2,1)S(1)}, u32[]{:S(2)}, u32[]{:S(2)}) collective-permute-start(bf16[2,512,256]{2,1,0:T(8,128)(2,1)S(1)} %pad_maximum_fusion.36), channel_id=1, source_target_pairs={{0,120},{8,128},{16,136},{24,144},{32,152},{40,160},{48,168},{56,1... | collective-permute-start | bytes 1572872 | tf_op jit(solution)/shard_map/ppermute | solution.py:12
  454.3 24.8 %collective-permute-start.23 = (bf16[2,512,256]{2,1,0:T(8,128)(2,1)S(1)}, bf16[2,512,256]{2,1,0:T(8,128)(2,1)S(1)}, u32[]{:S(2)}, u32[]{:S(2)}) collective-permute-start(bf16[2,512,256]{2,1,0:T(8,128)(2,1)S(1)} %pad_maximum_fusion.37), channel_id=1, source_target_pairs={{24,0},{32,8},{40,16},{48,24},{56,32},{64,40},{72,48},{80,56},{88,... | collective-permute-start | bytes 1572872 | tf_op jit(solution)/shard_map/ppermute | solution.py:12
  459.0 53.6 %collective-permute-start.24 = (bf16[2,512,256]{2,1,0:T(8,128)(2,1)S(1)}, bf16[2,512,256]{2,1,0:T(8,128)(2,1)S(1)}, u32[]{:S(2)}, u32[]{:S(2)}) collective-permute-start(bf16[2,512,256]{2,1,0:T(8,128)(2,1)S(1)} %pad_maximum_fusion.36), channel_id=1, source_target_pairs={{24,0},{32,8},{40,16},{48,24},{56,32},{64,40},{72,48},{80,56},{88,... | collective-permute-start | bytes 1572872 | tf_op jit(solution)/shard_map/ppermute | solution.py:12
  463.5 73.9 %collective-permute-start.22 = (bf16[2,512,256]{2,1,0:T(8,128)(2,1)S(1)}, bf16[2,512,256]{2,1,0:T(8,128)(2,1)S(1)}, u32[]{:S(2)}, u32[]{:S(2)}) collective-permute-start(bf16[2,512,256]{2,1,0:T(8,128)(2,1)S(1)} %pad_maximum_fusion.36), channel_id=1, source_target_pairs={{0,104},{8,112},{16,120},{24,128},{32,136},{40,144},{48,152},{56,1... | collective-permute-start | bytes 1572872 | tf_op jit(solution)/shard_map/ppermute | solution.py:12
  479.1 72.3 %collective-permute-start.27 = (bf16[2,512,256]{2,1,0:T(8,128)(2,1)S(1)}, bf16[2,512,256]{2,1,0:T(8,128)(2,1)S(1)}, u32[]{:S(2)}, u32[]{:S(2)}) collective-permute-start(bf16[2,512,256]{2,1,0:T(8,128)(2,1)S(1)} %pad_maximum_fusion.37), channel_id=1, source_target_pairs={{32,0},{40,8},{48,16},{56,24},{64,32},{72,40},{80,48},{88,56},{96,... | collective-permute-start | bytes 1572872 | tf_op jit(solution)/shard_map/ppermute | solution.py:12
  512.6 55.8 %collective-permute-start.28 = (bf16[2,512,256]{2,1,0:T(8,128)(2,1)S(1)}, bf16[2,512,256]{2,1,0:T(8,128)(2,1)S(1)}, u32[]{:S(2)}, u32[]{:S(2)}) collective-permute-start(bf16[2,512,256]{2,1,0:T(8,128)(2,1)S(1)} %pad_maximum_fusion.36), channel_id=1, source_target_pairs={{32,0},{40,8},{48,16},{56,24},{64,32},{72,40},{80,48},{88,56},{96,... | collective-permute-start | bytes 1572872 | tf_op jit(solution)/shard_map/ppermute | solution.py:12
  537.4 17.0 %collective-permute-start.21 = (bf16[2,512,256]{2,1,0:T(8,128)(2,1)S(1)}, bf16[2,512,256]{2,1,0:T(8,128)(2,1)S(1)}, u32[]{:S(2)}, u32[]{:S(2)}) collective-permute-start(bf16[2,512,256]{2,1,0:T(8,128)(2,1)S(1)} %pad_maximum_fusion.37), channel_id=1, source_target_pairs={{136,0},{144,8},{152,16},{160,24},{168,32},{176,40},{184,48},{192,... | collective-permute-start | bytes 1572872 | tf_op jit(solution)/shard_map/ppermute | solution.py:12
  551.4 34.9 %collective-permute-start.26 = (bf16[2,512,256]{2,1,0:T(8,128)(2,1)S(1)}, bf16[2,512,256]{2,1,0:T(8,128)(2,1)S(1)}, u32[]{:S(2)}, u32[]{:S(2)}) collective-permute-start(bf16[2,512,256]{2,1,0:T(8,128)(2,1)S(1)} %pad_maximum_fusion.36), channel_id=1, source_target_pairs={{0,96},{8,104},{16,112},{24,120},{32,128},{40,136},{48,144},{56,15... | collective-permute-start | bytes 1572872 | tf_op jit(solution)/shard_map/ppermute | solution.py:12
  554.4 16.9 %collective-permute-start.25 = (bf16[2,512,256]{2,1,0:T(8,128)(2,1)S(1)}, bf16[2,512,256]{2,1,0:T(8,128)(2,1)S(1)}, u32[]{:S(2)}, u32[]{:S(2)}) collective-permute-start(bf16[2,512,256]{2,1,0:T(8,128)(2,1)S(1)} %pad_maximum_fusion.37), channel_id=1, source_target_pairs={{152,0},{160,8},{168,16},{176,24},{184,32},{192,40},{200,48},{208,... | collective-permute-start | bytes 1572872 | tf_op jit(solution)/shard_map/ppermute | solution.py:12
  568.4 81.6 %collective-permute-start.31 = (bf16[2,512,256]{2,1,0:T(8,128)(2,1)S(1)}, bf16[2,512,256]{2,1,0:T(8,128)(2,1)S(1)}, u32[]{:S(2)}, u32[]{:S(2)}) collective-permute-start(bf16[2,512,256]{2,1,0:T(8,128)(2,1)S(1)} %pad_maximum_fusion.37), channel_id=1, source_target_pairs={{40,0},{48,8},{56,16},{64,24},{72,32},{80,40},{88,48},{96,56},{104... | collective-permute-start | bytes 1572872 | tf_op jit(solution)/shard_map/ppermute | solution.py:12
  571.4 18.0 %collective-permute-start.29 = (bf16[2,512,256]{2,1,0:T(8,128)(2,1)S(1)}, bf16[2,512,256]{2,1,0:T(8,128)(2,1)S(1)}, u32[]{:S(2)}, u32[]{:S(2)}) collective-permute-start(bf16[2,512,256]{2,1,0:T(8,128)(2,1)S(1)} %pad_maximum_fusion.37), channel_id=1, source_target_pairs={{160,0},{168,8},{176,16},{184,24},{192,32},{200,40},{208,48},{216,... | collective-permute-start | bytes 1572872 | tf_op jit(solution)/shard_map/ppermute | solution.py:12
  586.4 112.5 %collective-permute-start.32 = (bf16[2,512,256]{2,1,0:T(8,128)(2,1)S(1)}, bf16[2,512,256]{2,1,0:T(8,128)(2,1)S(1)}, u32[]{:S(2)}, u32[]{:S(2)}) collective-permute-start(bf16[2,512,256]{2,1,0:T(8,128)(2,1)S(1)} %pad_maximum_fusion.36), channel_id=1, source_target_pairs={{40,0},{48,8},{56,16},{64,24},{72,32},{80,40},{88,48},{96,56},{104... | collective-permute-start | bytes 1572872 | tf_op jit(solution)/shard_map/ppermute | solution.py:12
  589.4 113.7 %collective-permute-start.30 = (bf16[2,512,256]{2,1,0:T(8,128)(2,1)S(1)}, bf16[2,512,256]{2,1,0:T(8,128)(2,1)S(1)}, u32[]{:S(2)}, u32[]{:S(2)}) collective-permute-start(bf16[2,512,256]{2,1,0:T(8,128)(2,1)S(1)} %pad_maximum_fusion.36), channel_id=1, source_target_pairs={{0,88},{8,96},{16,104},{24,112},{32,120},{40,128},{48,136},{56,144... | collective-permute-start | bytes 1572872 | tf_op jit(solution)/shard_map/ppermute | solution.py:12
  645.1 35.9 %collective-permute-start.7 = (bf16[2,512,256]{2,1,0:T(8,128)(2,1)S(1)}, bf16[2,512,256]{2,1,0:T(8,128)(2,1)S(1)}, u32[]{:S(2)}, u32[]{:S(2)}) collective-permute-start(bf16[2,512,256]{2,1,0:T(8,128)(2,1)S(1)} %pad_maximum_fusion.37), channel_id=1, source_target_pairs={{96,0},{104,8},{112,16},{120,24},{128,32},{136,40},{144,48},{152,5... | collective-permute-start | bytes 1572872 | tf_op jit(solution)/shard_map/ppermute | solution.py:12
  648.1 67.8 %collective-permute-start.33 = (bf16[2,512,256]{2,1,0:T(8,128)(2,1)S(1)}, bf16[2,512,256]{2,1,0:T(8,128)(2,1)S(1)}, u32[]{:S(2)}, u32[]{:S(2)}) collective-permute-start(bf16[2,512,256]{2,1,0:T(8,128)(2,1)S(1)} %pad_maximum_fusion.37), channel_id=1, source_target_pairs={{168,0},{176,8},{184,16},{192,24},{200,32},{208,40},{216,48},{224,... | collective-permute-start | bytes 1572872 | tf_op jit(solution)/shard_map/ppermute | solution.py:12
  649.6 3.1 copy-start.54
  649.6 3.1 copy-start.79
  649.6 3.1 copy-start.90
  649.6 3.1 copy-start.91
  650.0 67.9 %collective-permute-start.3 = (bf16[2,512,256]{2,1,0:T(8,128)(2,1)S(1)}, bf16[2,512,256]{2,1,0:T(8,128)(2,1)S(1)}, u32[]{:S(2)}, u32[]{:S(2)}) collective-permute-start(bf16[2,512,256]{2,1,0:T(8,128)(2,1)S(1)} %pad_maximum_fusion.37), channel_id=1, source_target_pairs={{88,0},{96,8},{104,16},{112,24},{120,32},{128,40},{136,48},{144,56... | collective-permute-start | bytes 1572872 | tf_op jit(solution)/shard_map/ppermute | solution.py:12
  653.1 42.3 %copy-start.65 = (pred[1536]{0:T(1024)(128)(4,1)S(1)}, pred[1536]{0:T(1024)(128)(4,1)}, u32[]{:S(2)}) copy-start(pred[1536]{0:T(1024)(128)(4,1)} %get-tuple-element.274) | copy-start | bytes 4612
  653.1 42.3 %copy-start.66 = (pred[1536]{0:T(1024)(128)(4,1)S(1)}, pred[1536]{0:T(1024)(128)(4,1)}, u32[]{:S(2)}) copy-start(pred[1536]{0:T(1024)(128)(4,1)} %get-tuple-element.276) | copy-start | bytes 4612
  653.1 42.3 %copy-start.76 = (pred[1536]{0:T(1024)(128)(4,1)S(1)}, pred[1536]{0:T(1024)(128)(4,1)}, u32[]{:S(2)}) copy-start(pred[1536]{0:T(1024)(128)(4,1)} %get-tuple-element.279) | copy-start | bytes 4612
  653.1 42.3 %copy-start.77 = (pred[1536]{0:T(1024)(128)(4,1)S(1)}, pred[1536]{0:T(1024)(128)(4,1)}, u32[]{:S(2)}) copy-start(pred[1536]{0:T(1024)(128)(4,1)} %get-tuple-element.277) | copy-start | bytes 4612
  653.1 42.3 %copy-start.78 = (pred[1536]{0:T(1024)(128)(4,1)S(1)}, pred[1536]{0:T(1024)(128)(4,1)}, u32[]{:S(2)}) copy-start(pred[1536]{0:T(1024)(128)(4,1)} %get-tuple-element.275) | copy-start | bytes 4612
  653.1 42.3 %copy-start.88 = (pred[64]{0:T(512)(128)(4,1)S(1)}, pred[64]{0:T(512)(128)(4,1)}, u32[]{:S(2)}) copy-start(pred[64]{0:T(512)(128)(4,1)} %get-tuple-element.293) | copy-start | bytes 196
  653.1 42.3 %copy-start.89 = (s32[64]{0:T(128)S(1)}, s32[64]{0:T(128)}, u32[]{:S(2)}) copy-start(s32[64]{0:T(128)} %get-tuple-element.287) | copy-start | bytes 772
  681.0 39.0 %collective-permute-start.15 = (bf16[2,512,256]{2,1,0:T(8,128)(2,1)S(1)}, bf16[2,512,256]{2,1,0:T(8,128)(2,1)S(1)}, u32[]{:S(2)}, u32[]{:S(2)}) collective-permute-start(bf16[2,512,256]{2,1,0:T(8,128)(2,1)S(1)} %pad_maximum_fusion.37), channel_id=1, source_target_pairs={{120,0},{128,8},{136,16},{144,24},{152,32},{160,40},{168,48},{176,... | collective-permute-start | bytes 1572872 | tf_op jit(solution)/shard_map/ppermute | solution.py:12
  698.8 25.8 %collective-permute-start.17 = (bf16[2,512,256]{2,1,0:T(8,128)(2,1)S(1)}, bf16[2,512,256]{2,1,0:T(8,128)(2,1)S(1)}, u32[]{:S(2)}, u32[]{:S(2)}) collective-permute-start(bf16[2,512,256]{2,1,0:T(8,128)(2,1)S(1)} %pad_maximum_fusion.37), channel_id=1, source_target_pairs={{128,0},{136,8},{144,16},{152,24},{160,32},{168,40},{176,48},{184,... | collective-permute-start | bytes 1572872 | tf_op jit(solution)/shard_map/ppermute | solution.py:12
  703.1 11.9 %copy-start.69 = (pred[1536]{0:T(1024)(128)(4,1)S(1)}, pred[1536]{0:T(1024)(128)(4,1)}, u32[]{:S(2)}) copy-start(pred[1536]{0:T(1024)(128)(4,1)} %get-tuple-element.272) | copy-start | bytes 4612
  703.1 23.8 %collective-permute-start.11 = (bf16[2,512,256]{2,1,0:T(8,128)(2,1)S(1)}, bf16[2,512,256]{2,1,0:T(8,128)(2,1)S(1)}, u32[]{:S(2)}, u32[]{:S(2)}) collective-permute-start(bf16[2,512,256]{2,1,0:T(8,128)(2,1)S(1)} %pad_maximum_fusion.37), channel_id=1, source_target_pairs={{104,0},{112,8},{120,16},{128,24},{136,32},{144,40},{152,48},{160,... | collective-permute-start | bytes 1572872 | tf_op jit(solution)/shard_map/ppermute | solution.py:12
  736.9 2.5 copy-start.5
  760.8 75.7 %copy-start.2 = (bf16[512,4,256]{2,0,1:T(8,128)(2,1)S(1)}, bf16[512,4,256]{2,0,1:T(8,128)(2,1)}, u32[]{:S(2)}) copy-start(bf16[512,4,256]{2,0,1:T(8,128)(2,1)} %all-gather.3.cloned.1.call-done) | copy-start | bytes 3145732
  760.8 75.7 %copy-start.33 = (bf16[128,256]{1,0:T(8,128)(2,1)S(1)}, bf16[128,256]{1,0:T(8,128)(2,1)}, u32[]{:S(2)}) copy-start(bf16[128,256]{1,0:T(8,128)(2,1)} %param.8) | copy-start | bytes 196612
  763.1 164.9 %all-reduce.4.cloned.1.call-start = ((), (), s32[]{:S(2)}) async-start(), calls=%async_computation.4 | async-start | bytes 524288 | tf_op jit(solution)/shard_map/psum | solution.py:180
  764.1 387.8 %all-reduce.6.cloned.1.call-start = ((), (), s32[]{:S(2)}) async-start(), calls=%async_computation.5 | async-start | bytes 1048576 | tf_op jit(solution)/shard_map/psum | solution.py:179
  (69 other events, 85.5 us)
Sparse Core Ops, SparseCore 0:
  11.2 53.4 all-gather.2
  73.0 82.5 reduce-scatter.1
  763.2 73.2 all-gather.4
  839.6 88.3 all-reduce.3
  931.4 220.4 all-reduce.5
